TPU v7x, 128 devices: a whole 4x4x4 slice. The times are simulated.
128 devices in a mesh: tx: 16 (over x, y), ty: 8 (over z, core).
Axes of the slice: x: 4, y: 4, z: 4, core: 2. Of those that a mesh axis runs over, the one named last changes fastest.
Arguments:
- object_field: float32 [2, 8192, 4096], P(None, 'tx', 'ty'), may hold values from -5 to 5
- probe_field: float32 [2, 256, 256], replicated, may hold values from -5 to 5
- amplitudes: float32 [768, 2048, 256], P('tx', 'ty'), may hold values from 0.3 to 3
- scan_blocks: int32 [2048, 2], P(('tx', 'ty')), may hold values from 0 to 63, as said below
- owner_rows: int32 [2048], P(('tx', 'ty')), may hold values from 0 to 15, as said below
Outputs:
- refined_object: float32 [2, 8192, 4096], P(None, 'tx', 'ty')
Inputs may be any that keep to these rules, and one draw needn't show every extreme that they name: `scan_blocks`: position p has home device p // 16 in tx-major order; its block row lies within that device's 512 rows divided by 128, its block column within its 512 columns divided by 128. `owner_rows`: of one home device's positions at most 3 share an owner, and in every ty column some home device has exactly 3 positions with the same owner; one owner holds at most 40 positions, and some hold exactly that many.
All inputs are finite; a program needn't handle non-finite values.
Results may differ from a plain program's by a relative error of at most 0.0042.
Values may be sent and summed in bfloat16 or wider, within the bound.
A program may use at most 128 MiB of HBM per device.

v0:
```python
import jax
import jax.numpy as jnp
from jax import lax
from jax.sharding import PartitionSpec as P

STEPS = 4


KAPPA_SQ = 1.0
TIME_STEP = 0.2
AMPLITUDE_FLOOR = 0.5


def from_behind(value, axis, steps):
    count = lax.axis_size(axis)
    initial, last = (max(0, -steps), min(count, count - steps))
    return lax.ppermute(value, axis, [(source, source + steps) for source in range(initial, last)])


def extended_2(array, sides, width):
    for axis, dim in sides:
        peers, length = (lax.axis_size(axis), array.shape[dim])
        up = [(i, (i + 1) % peers) for i in range(peers - 1)]
        down = [(j, i) for i, j in up]
        last = lax.slice_in_dim(array, length - width, length, axis=dim)
        initial = lax.slice_in_dim(array, 0, width, axis=dim)
        before = lax.ppermute(last, axis, up)
        after = lax.ppermute(initial, axis, down)
        array = jnp.concatenate([before, array, after], axis=dim)
    return array


def dft_tables(window_cells):
    counter = jnp.arange(window_cells, dtype=jnp.int32)
    phases = counter[:, None] * counter[None, :] % window_cells
    angles = phases.astype(jnp.float32) * (2.0 * jnp.pi / window_cells)
    scaling = 1.0 / jnp.sqrt(jnp.asarray(window_cells, jnp.float32))
    return (
        (jnp.cos(angles) * scaling).astype(jnp.bfloat16),
        (jnp.sin(angles) * scaling).astype(jnp.bfloat16),
    )


def left_product(table, values):
    return jnp.einsum("jk,nkl->njl", table, values, preferred_element_type=jnp.float32)


def right_product(values, table):
    return jnp.einsum("njk,kl->njl", values, table, preferred_element_type=jnp.float32)


def batch_left(cosine, sine, real_part, imag_part, signum):
    return (
        left_product(cosine, real_part) + signum * left_product(sine, imag_part),
        left_product(cosine, imag_part) - signum * left_product(sine, real_part),
    )


def batch_right(cosine, sine, real_part, imag_part, signum):
    return (
        right_product(real_part, cosine) + signum * right_product(imag_part, sine),
        right_product(imag_part, cosine) - signum * right_product(real_part, sine),
    )


def batch_gradient(exit_waves, measured, probe_field, cosine, sine):
    probe_re = probe_field[0]
    probe_im = probe_field[1]
    half_re, half_im = batch_left(cosine, sine, exit_waves[:, 0], exit_waves[:, 1], 1.0)
    far_re, far_im = batch_right(
        cosine, sine, half_re.astype(jnp.bfloat16), half_im.astype(jnp.bfloat16), 1.0
    )
    magnitude = jnp.sqrt(far_re * far_re + far_im * far_im)
    factor = 1.0 - measured / jnp.maximum(magnitude, AMPLITUDE_FLOOR)
    back_re, back_im = batch_left(
        cosine,
        sine,
        (far_re * factor).astype(jnp.bfloat16),
        (far_im * factor).astype(jnp.bfloat16),
        -1.0,
    )
    near_re, near_im = batch_right(
        cosine, sine, back_re.astype(jnp.bfloat16), back_im.astype(jnp.bfloat16), -1.0
    )
    grad_re = (probe_re * near_re + probe_im * near_im).astype(jnp.bfloat16)
    grad_im = (probe_re * near_im - probe_im * near_re).astype(jnp.bfloat16)
    return jnp.stack([grad_re, grad_im], axis=1)


def process_batches(exit_waves, measured, probe_field, cosine, sine):
    return lax.map(
        lambda paired: batch_gradient(paired[0], paired[1], probe_field, cosine, sine),
        (exit_waves, measured),
    )


def smooth_pass(padded):
    center = padded[:, 1:-1, 1:-1]
    flux_sum = jnp.zeros_like(center)
    for neighbour in (
        padded[:, :-2, 1:-1],
        padded[:, 2:, 1:-1],
        padded[:, 1:-1, :-2],
        padded[:, 1:-1, 2:],
    ):
        difference = neighbour - center
        weight = 1.0 / (
            1.0 + (difference[0] * difference[0] + difference[1] * difference[1]) / KAPPA_SQ
        )
        flux_sum = flux_sum + weight * difference
    return center + TIME_STEP * flux_sum


def local(object_field, probe_field, amplitudes, scan_blocks, owner_rows):
    tile_rows = object_field.shape[1]
    tile_cols = object_field.shape[2]
    window_cells = probe_field.shape[1]
    block_cells = window_cells // 2
    positions_here = owner_rows.shape[0]
    groups = lax.axis_size("tx")
    pair_slots = amplitudes.shape[0] // groups
    slot_total = groups * pair_slots
    plane_cells = 2 * window_cells * window_cells
    row_index = lax.axis_index("tx")
    col_index = lax.axis_index("ty")
    anchor = jnp.zeros((), jnp.int32)
    cosine, sine = dft_tables(window_cells)
    probe_re = probe_field[0]
    probe_im = probe_field[1]
    lower_rows = from_behind(object_field[:, :block_cells, :], "tx", -1)
    taller = jnp.concatenate([object_field, lower_rows], axis=1)
    right_cols = from_behind(taller[:, :, :block_cells], "ty", -1)
    extended = jnp.concatenate([taller, right_cols], axis=2)
    local_rows = scan_blocks[:, 0] * block_cells - row_index * tile_rows
    local_cols = scan_blocks[:, 1] * block_cells - col_index * tile_cols

    def cut_window(start_row, start_col):
        return lax.dynamic_slice(
            extended, (anchor, start_row, start_col), (2, window_cells, window_cells)
        )

    windows = jax.vmap(cut_window)(local_rows, local_cols)
    exit_waves = jnp.stack(
        [
            probe_re * windows[:, 0] - probe_im * windows[:, 1],
            probe_re * windows[:, 1] + probe_im * windows[:, 0],
        ],
        axis=1,
    ).astype(jnp.bfloat16)
    earlier_mask = jnp.arange(positions_here)[None, :] < jnp.arange(positions_here)[:, None]
    same_owner = owner_rows[:, None] == owner_rows[None, :]
    pair_rank = jnp.sum(same_owner & earlier_mask, axis=1)
    slot_index = owner_rows * pair_slots + pair_rank
    selector = (jnp.arange(slot_total, dtype=jnp.int32)[:, None] == slot_index[None, :]).astype(
        jnp.bfloat16
    )
    flattened = exit_waves.reshape(positions_here, plane_cells)
    outgoing = jnp.dot(selector, flattened, preferred_element_type=jnp.float32).astype(jnp.bfloat16)
    outgoing = outgoing.reshape(slot_total, 2, window_cells, window_cells)
    incoming = lax.all_to_all(outgoing, "tx", split_axis=0, concat_axis=0, tiled=True)
    gradients = process_batches(
        incoming.reshape(groups, pair_slots, 2, window_cells, window_cells),
        amplitudes.reshape(groups, pair_slots, window_cells, window_cells),
        probe_field,
        cosine,
        sine,
    )
    returned = lax.all_to_all(
        gradients.reshape(slot_total, 2, window_cells, window_cells),
        "tx",
        split_axis=0,
        concat_axis=0,
        tiled=True,
    )
    own_grads = jnp.dot(
        selector.T, returned.reshape(slot_total, plane_cells), preferred_element_type=jnp.float32
    )
    own_grads = own_grads.reshape(positions_here, 2, window_cells, window_cells)
    illumination_window = probe_re * probe_re + probe_im * probe_im

    def deposit_one(number, accumulated):
        gradient_sum, illumination = accumulated
        start_row = local_rows[number]
        start_col = local_cols[number]
        region = lax.dynamic_slice(
            gradient_sum, (anchor, start_row, start_col), (2, window_cells, window_cells)
        )
        gradient_sum = lax.dynamic_update_slice(
            gradient_sum, region + own_grads[number], (anchor, start_row, start_col)
        )
        lit_region = lax.dynamic_slice(
            illumination, (start_row, start_col), (window_cells, window_cells)
        )
        illumination = lax.dynamic_update_slice(
            illumination, lit_region + illumination_window, (start_row, start_col)
        )
        return (gradient_sum, illumination)

    initial = (
        jnp.zeros((2, tile_rows + block_cells, tile_cols + block_cells), jnp.float32),
        jnp.zeros((tile_rows + block_cells, tile_cols + block_cells), jnp.float32),
    )
    gradient_sum, illumination = lax.fori_loop(0, positions_here, deposit_one, initial)
    from_above = (
        from_behind(gradient_sum[:, tile_rows:, :].astype(jnp.bfloat16), "tx", 1).astype(
            jnp.float32
        ),
        from_behind(illumination[tile_rows:, :].astype(jnp.bfloat16), "tx", 1).astype(jnp.float32),
    )
    grad_top = gradient_sum[:, :tile_rows, :].at[:, :block_cells, :].add(from_above[0])
    light_top = illumination[:tile_rows, :].at[:block_cells, :].add(from_above[1])
    from_left = (
        from_behind(grad_top[:, :, tile_cols:].astype(jnp.bfloat16), "ty", 1).astype(jnp.float32),
        from_behind(light_top[:, tile_cols:].astype(jnp.bfloat16), "ty", 1).astype(jnp.float32),
    )
    grad_tile = grad_top[:, :, :tile_cols].at[:, :, :block_cells].add(from_left[0])
    light_tile = light_top[:, :tile_cols].at[:, :block_cells].add(from_left[1])
    updated = object_field - grad_tile / (light_tile + 1.0)
    for number in range(STEPS):
        padded = extended_2(updated, (("tx", 1), ("ty", 2)), 1)
        updated = smooth_pass(padded)
    return updated


def solution(mesh):
    in_specs = (
        P(None, "tx", "ty"),
        P(),
        P("tx", "ty", None),
        P(("tx", "ty"), None),
        P(("tx", "ty")),
    )
    out_specs = P(None, "tx", "ty")
    return jax.shard_map(local, mesh=mesh, in_specs=in_specs, out_specs=out_specs, check_vma=False)
```

profile of v0, /device:TPU:7, one launch (start us, length us, event | category | flops | bytes accessed | tf_op | source)
XLA Modules:
  0.0 1396.3 jit_solution(10063251086817947481)
XLA Ops:
  7.9 8.7 collective-permute-done
  21.1 8.8 collective-permute-done.1
  30.2 44.9 %while.33 = (s32[]{:T(128)}, f32[2,640,640]{2,1,0:T(8,128)S(1)}, s32[16,3]{0,1:T(4,128)S(1)}, f32[16,2,256,256]{3,2,1,0:T(8,128)}, s32[]{:T(128)}) while((s32[]{:T(128)}, f32[2,640,640]{2,1,0:T(8,128)S(1)}, s32[16,3]{0,1:T(4,128)S(1)}, f32[16,2,256,256]{3,2,1,0:T(8,128)}, s32[]{:T(128)}) %tuple.122), condition=%wide.while_cond.4, body=%wide.while_body.4.sunk | while | flops 2 | bytes 1050217 | solution.py:138
  84.7 5.7 convolution_convert_fusion
  90.4 6.0 copy.139
  96.4 8.1 all-to-all-start
  104.5 165.6 %all-to-all-done = bf16[48,2,256,256]{3,2,1,0:T(8,128)(2,1)} async-done(((bf16[48,2,256,256]{3,2,1,0:T(8,128)(2,1)}), bf16[48,2,256,256]{3,2,1,0:T(8,128)(2,1)}, u32[]{:S(2)}, u32[]{:S(2)}) %all-to-all-start) | async-done | bytes 12582944 | tf_op jit(solution)/shard_map/all_to_all | solution.py:160
  270.1 388.0 %while.34 = (s32[]{:T(128)}, bf16[16,3,2,256,256]{4,3,2,1,0:T(8,128)(2,1)}, f32[2,256,256]{2,1,0:T(8,128)S(1)}, bf16[16,3,2,256,256]{4,3,2,1,0:T(8,128)(2,1)}, f32[16,3,256,256]{3,2,1,0:T(8,128)}, /*index=5*/s32[]{:T(128)}) while((s32[]{:T(128)}, bf16[16,3,2,256,256]{4,3,2,1,0:T(8,128)(2,1)}, ...), condition=%wide.region_2.3_spmd.clone.clone, body=%wide.region_1.2_spmd.clone.clone.sunk | while | flops 1634467840 | bytes 32244300 | solution.py:91
  658.1 14.3 %all-to-all-start.1 = ((bf16[48,2,256,256]{3,2,1,0:T(8,128)(2,1)}), bf16[48,2,256,256]{3,2,1,0:T(8,128)(2,1)}, u32[]{:S(2)}, u32[]{:S(2)}) async-start(bf16[48,2,256,256]{3,2,1,0:T(8,128)(2,1)} %bitcast.11), calls=%async_computation.1 | async-start | bytes 25165824 | tf_op jit(solution)/shard_map/all_to_all | solution.py:168
  672.5 145.6 %all-to-all-done.1 = bf16[48,2,256,256]{3,2,1,0:T(8,128)(2,1)} async-done(((bf16[48,2,256,256]{3,2,1,0:T(8,128)(2,1)}), bf16[48,2,256,256]{3,2,1,0:T(8,128)(2,1)}, u32[]{:S(2)}, u32[]{:S(2)}) %all-to-all-start.1) | async-done | bytes 12582944 | tf_op jit(solution)/shard_map/all_to_all | solution.py:168
  818.0 14.8 %fusion.132 = f32[16,2,256,256]{3,0,2,1:T(8,128)} fusion(bf16[2,256,256,48]{2,1,0,3:T(8,128)(2,1)} %bitcast.61, s32[16]{0:T(128)S(1)} %multiply_add_fusion.5), kind=kOutput, calls=%fused_computation.145 | convolution fusion | flops 201327360 | bytes 20971584 | tf_op jit(solution)/shard_map/dot_general | solution.py:175
  834.8 287.2 %while.32 = (s32[]{:T(128)}, f32[2,640,640]{2,1,0:T(8,128)}, f32[640,640]{1,0:T(8,128)S(1)}, s32[16]{0:T(128)S(1)}, s32[16]{0:T(128)S(1)}, /*index=5*/f32[16,2,2...) while((s32[]{:T(128)}, f32[2,640,640]{2,1,0:T(8,128)}, ...), condition=%wide.region_4.5_spmd, body=%wide.region_3.4_spmd.sunk | while | flops 196616 | bytes 4980957 | solution.py:203
  843.7 5.9 dynamic_update_slice.24
  863.3 5.2 dynamic_update_slice.24
  897.4 5.8 dynamic_update_slice.24
  916.1 5.9 dynamic_update_slice.24
  935.8 5.2 dynamic_update_slice.24
  952.9 5.2 dynamic_update_slice.24
  986.3 5.7 dynamic_update_slice.24
  1021.8 5.9 dynamic_update_slice.24
  1041.5 5.2 dynamic_update_slice.24
  1075.5 5.8 dynamic_update_slice.24
  1111.1 5.9 dynamic_update_slice.24
  1124.4 6.2 collective-permute-done.4
  1130.6 143.1 %collective-permute-start.5 = (bf16[512,128]{1,0:T(8,128)(2,1)S(1)}, bf16[512,128]{1,0:T(8,128)(2,1)S(1)}, u32[]{:S(2)}, u32[]{:S(2)}) collective-permute-start(bf16[512,128]{1,0:T(8,128)(2,1)S(1)} %slice.787), channel_id=1, source_target_pairs={{0,1},{1,2},{2,3},{3,4},{4,5},{5,6},{6,7},{8,9},{9,10},{10,11},{11... | collective-permute-start | bytes 393224 | tf_op jit(solution)/shard_map/ppermute | solution.py:17
  1277.3 8.3 collective-permute-done.2
  1294.4 5.7 collective-permute-start.7
  1301.1 5.5 collective-permute-start.8
  1320.9 6.0 collective-permute-start.11
  1328.2 5.5 collective-permute-start.12
  1347.9 6.0 collective-permute-start.15
  1372.4 6.0 collective-permute-start.19
  (606 shorter events, 693.6 us)
Async XLA Ops:
  1.1 15.5 %collective-permute-start = (f32[2,128,512]{2,1,0:T(8,128)S(1)}, f32[2,128,512]{2,1,0:T(8,128)S(1)}, u32[]{:S(2)}, u32[]{:S(2)}) collective-permute-start(f32[2,128,512]{2,1,0:T(8,128)S(1)} %slice.399), channel_id=1, source_target_pairs={{8,0},{16,8},{24,16},{32,24},{40,32},{48,40},{56,48},{64,56},{72,6... | collective-permute-start | bytes 1572872 | tf_op jit(solution)/shard_map/ppermute | solution.py:17
  7.8 12.4 copy-start.11
  7.8 12.6 copy-start.7
  16.7 13.2 collective-permute-start.1
  96.4 173.7 %copy-start.8 = (f32[2,256,256]{2,1,0:T(8,128)S(1)}, f32[2,256,256]{2,1,0:T(8,128)}, u32[]{:S(2)}) copy-start(f32[2,256,256]{2,1,0:T(8,128)} %param.18) | copy-start | bytes 1572868
  96.4 173.7 %all-to-all-start = ((bf16[48,2,256,256]{3,2,1,0:T(8,128)(2,1)}), bf16[48,2,256,256]{3,2,1,0:T(8,128)(2,1)}, u32[]{:S(2)}, u32[]{:S(2)}) async-start(bf16[48,2,256,256]{3,2,1,0:T(8,128)(2,1)} %bitcast.246), calls=%async_computation | async-start | bytes 25165824 | tf_op jit(solution)/shard_map/all_to_all | solution.py:160
  658.1 159.9 %all-to-all-start.1 = ((bf16[48,2,256,256]{3,2,1,0:T(8,128)(2,1)}), bf16[48,2,256,256]{3,2,1,0:T(8,128)(2,1)}, u32[]{:S(2)}, u32[]{:S(2)}) async-start(bf16[48,2,256,256]{3,2,1,0:T(8,128)(2,1)} %bitcast.11), calls=%async_computation.1 | async-start | bytes 25165824 | tf_op jit(solution)/shard_map/all_to_all | solution.py:168
  1122.0 151.6 %copy-start.6 = (f32[2,640,640]{2,1,0:T(8,128)S(1)}, f32[2,640,640]{2,1,0:T(8,128)}, u32[]{:S(2)}) copy-start(f32[2,640,640]{2,1,0:T(8,128)} %get-tuple-element.258) | copy-start | bytes 9830404
  1122.1 8.4 collective-permute-start.4
  1130.6 146.0 %collective-permute-start.5 = (bf16[512,128]{1,0:T(8,128)(2,1)S(1)}, bf16[512,128]{1,0:T(8,128)(2,1)S(1)}, u32[]{:S(2)}, u32[]{:S(2)}) collective-permute-start(bf16[512,128]{1,0:T(8,128)(2,1)S(1)} %slice.787), channel_id=1, source_target_pairs={{0,1},{1,2},{2,3},{3,4},{4,5},{5,6},{6,7},{8,9},{9,10},{10,11},{11... | collective-permute-start | bytes 393224 | tf_op jit(solution)/shard_map/ppermute | solution.py:17
  1273.7 11.9 collective-permute-start.2
  1285.7 6.1 collective-permute-start.3
  1292.5 7.6 collective-permute-start.6
  1294.4 6.2 collective-permute-start.7
  1301.1 7.7 collective-permute-start.8
  1306.8 4.9 collective-permute-start.9
  1319.0 8.7 copy-start
  1319.0 8.0 collective-permute-start.10
  1320.9 6.8 collective-permute-start.11
  1327.9 11.1 copy-start.1
  1328.2 7.6 collective-permute-start.12
  1333.8 4.9 collective-permute-start.13
  1346.0 8.7 copy-start.2
  1346.0 8.0 collective-permute-start.14
  1347.9 6.8 collective-permute-start.15
  1355.1 5.3 collective-permute-start.16
  1358.3 4.9 collective-permute-start.17
  1370.4 8.7 copy-start.4
  1370.5 8.0 collective-permute-start.18
  1372.4 6.8 collective-permute-start.19
  1379.6 5.1 collective-permute-start.20
  1382.8 4.9 collective-permute-start.21
  (4 other events, 22.2 us)
where the time goes:
time: 1410 us; the launch traced here: 1400 us
  waiting for transfers between devices  360 us (26%)
  matrix products  359 us (25%)
  local copies, waits for them, and re-layouts  294 us (21%)
  starting transfers between devices  237 us (17%)
  other arithmetic  76.4 us (5%)
  loops' own time  69.8 us (5%)
    dot_general x128, matrix products, right_product(): jnp.einsum('njk,kl->njl', values, table, preferred_element_type=jnp.float32)  183 us
    all_to_all x1, waiting for transfers between devices, local(): lax.all_to_all(outgoing, 'tx', split_axis=0, concat_axis=0, tiled=True)  166 us
    ppermute x6, starting transfers between devices, from_behind(): lax.ppermute(value, axis, [(source, source + steps) for source in range(i...  158 us
    dot_general x128, matrix products, left_product(): jnp.einsum('jk,nkl->njl', table, values, preferred_element_type=jnp.float32)  155 us
    all_to_all x1, waiting for transfers between devices, local(): lax.all_to_all(gradients.reshape(slot_total, 2, window_cells, window_cell...  146 us
    dynamic_update_slice x16, local copies, waits for them, and re-layouts, deposit_one(): lax.dynamic_update_slice(gradient_sum, region + own_grads[number], (ancho...  85.4 us
    another operation x1, loops' own time, local(): lax.fori_loop(0, positions_here, deposit_one, initial)  59.1 us
    dynamic_update_slice x16, local copies, waits for them, and re-layouts, deposit_one(): lax.dynamic_update_slice(illumination, lit_region + illumination_window,...  58.1 us
  transfers between devices with their start and end apart: 24, of which 15 were waited for; matrix products, arithmetic and copies ran while one was open for 0% of the time, Pallas kernels for 0%

commit v1 on v0

v1 whole, which is shorter than its diff:
```python
import functools

import jax
import jax.numpy as jnp
import numpy as np
from jax import lax
from jax.experimental import pallas as pl
from jax.experimental.pallas import tpu as pltpu
from jax.sharding import PartitionSpec as P

STEPS = 4


KAPPA_SQ = 1.0
TIME_STEP = 0.2
AMPLITUDE_FLOOR = 0.5


def from_behind(value, axis, steps):
    count = lax.axis_size(axis)
    initial, last = (max(0, -steps), min(count, count - steps))
    return lax.ppermute(value, axis, [(source, source + steps) for source in range(initial, last)])


def extended_2(array, sides, width):
    for axis, dim in sides:
        peers, length = (lax.axis_size(axis), array.shape[dim])
        up = [(i, (i + 1) % peers) for i in range(peers - 1)]
        down = [(j, i) for i, j in up]
        last = lax.slice_in_dim(array, length - width, length, axis=dim)
        initial = lax.slice_in_dim(array, 0, width, axis=dim)
        before = lax.ppermute(last, axis, up)
        after = lax.ppermute(initial, axis, down)
        array = jnp.concatenate([before, array, after], axis=dim)
    return array


def complex_tables(window_cells):
    counter = np.arange(window_cells)
    phases = counter[:, None] * counter[None, :] % window_cells
    angles = phases.astype(np.float32) * np.float32(2.0 * np.pi / window_cells)
    scaling = np.float32(1.0 / np.sqrt(window_cells))
    cosine, sine = (np.cos(angles) * scaling, np.sin(angles) * scaling)
    ahead = np.block([[cosine, sine], [-sine, cosine]])
    conjugate = np.block([[cosine, -sine], [sine, cosine]])
    return jnp.asarray(ahead, jnp.bfloat16), jnp.asarray(conjugate, jnp.bfloat16)


def matmul(first, second):
    return jnp.dot(first, second, preferred_element_type=jnp.float32)


def corner_of(number, spots, cells):
    start_row = pl.multiple_of(number // spots * cells, cells)
    start_col = pl.multiple_of(number % spots * cells, cells)
    return start_row, start_col


def forward_kernel(spots, extended, probe, ahead, conjugate, far_out, phase_out):
    cells = probe.shape[1]
    start_row, start_col = corner_of(pl.program_id(0), spots, cells // 2)
    view = (pl.ds(start_row, cells), pl.ds(start_col, cells))
    window_re, window_im = extended[(0, *view)], extended[(1, *view)]
    probe_re, probe_im = probe[0], probe[1]
    wave_re = (probe_re * window_re - probe_im * window_im).astype(jnp.bfloat16)
    wave_im = (probe_re * window_im + probe_im * window_re).astype(jnp.bfloat16)
    half = matmul(ahead[...], jnp.concatenate([wave_re, wave_im], axis=0)).astype(jnp.bfloat16)
    far = matmul(jnp.concatenate([half[:cells], half[cells:]], axis=1), conjugate[...])
    far_re, far_im = far[:, :cells], far[:, cells:]
    inverse = jnp.minimum(
        lax.rsqrt(far_re * far_re + far_im * far_im), 1.0 / AMPLITUDE_FLOOR
    )
    far_out[0, 0] = far_re.astype(jnp.bfloat16)
    far_out[0, 1] = far_im.astype(jnp.bfloat16)
    phase_out[0, 0] = (far_re * inverse).astype(jnp.bfloat16)
    phase_out[0, 1] = (far_im * inverse).astype(jnp.bfloat16)


def backward_kernel(
    spots, slots, starts, far, phase, arrived, probe, ahead, conjugate, grads, light, measured
):
    cells = probe.shape[1]
    number = pl.program_id(0)

    @pl.when(number == 0)
    def _():
        grads[...] = jnp.zeros_like(grads)
        light[...] = jnp.zeros_like(light)

    first, last = starts[number], starts[number + 1]

    @pl.when(last > first)
    def _():
        measured[...] = arrived[slots[first]].astype(jnp.float32)

        def add_one(index, carry):
            measured[...] += arrived[slots[index]].astype(jnp.float32)
            return carry

        lax.fori_loop(first + 1, last, add_one, 0)
        count = (last - first).astype(jnp.float32)
        total = measured[...]
        residual = [
            (far[0, part].astype(jnp.float32) * count
             - phase[0, part].astype(jnp.float32) * total).astype(jnp.bfloat16)
            for part in range(2)
        ]
        back = matmul(conjugate[...], jnp.concatenate(residual, axis=0)).astype(jnp.bfloat16)
        near = matmul(jnp.concatenate([back[:cells], back[cells:]], axis=1), ahead[...])
        near_re, near_im = near[:, :cells], near[:, cells:]
        probe_re, probe_im = probe[0], probe[1]
        start_row, start_col = corner_of(number, spots, cells // 2)
        view = (pl.ds(start_row, cells), pl.ds(start_col, cells))
        grads[(0, *view)] += probe_re * near_re + probe_im * near_im
        grads[(1, *view)] += probe_re * near_im - probe_im * near_re
        light[view] += count * (probe_re * probe_re + probe_im * probe_im)


def whole(shape):
    return pl.BlockSpec(shape, lambda *_: (0,) * len(shape))


def smooth_pass(padded):
    center = padded[:, 1:-1, 1:-1]
    flux_sum = jnp.zeros_like(center)
    for neighbour in (
        padded[:, :-2, 1:-1],
        padded[:, 2:, 1:-1],
        padded[:, 1:-1, :-2],
        padded[:, 1:-1, 2:],
    ):
        difference = neighbour - center
        weight = 1.0 / (
            1.0 + (difference[0] * difference[0] + difference[1] * difference[1]) / KAPPA_SQ
        )
        flux_sum = flux_sum + weight * difference
    return center + TIME_STEP * flux_sum


def local(object_field, probe_field, amplitudes, scan_blocks, owner_rows):
    tile_rows, tile_cols = object_field.shape[1:]
    window_cells = probe_field.shape[1]
    block_cells = window_cells // 2
    positions_here = owner_rows.shape[0]
    pair_slots = amplitudes.shape[0] // lax.axis_size("tx")
    spots = tile_cols // block_cells
    windows = tile_rows // block_cells * spots
    ext_rows, ext_cols = tile_rows + block_cells, tile_cols + block_cells

    arrived = lax.all_to_all(
        amplitudes.astype(jnp.bfloat16), "tx", split_axis=0, concat_axis=0, tiled=True
    )

    lower_rows = from_behind(object_field[:, :block_cells, :], "tx", -1)
    taller = jnp.concatenate([object_field, lower_rows], axis=1)
    right_cols = from_behind(taller[:, :, :block_cells], "ty", -1)
    extended = jnp.concatenate([taller, right_cols], axis=2)

    order = jnp.arange(positions_here, dtype=jnp.int32)
    earlier = order[None, :] < order[:, None]
    pair_rank = jnp.sum((owner_rows[:, None] == owner_rows[None, :]) & earlier, axis=1)
    slot_index = owner_rows * pair_slots + pair_rank.astype(jnp.int32)
    window_index = (
        (scan_blocks[:, 0] - lax.axis_index("tx") * (tile_rows // block_cells)) * spots
        + scan_blocks[:, 1] - lax.axis_index("ty") * spots
    )
    before = (window_index[None, :] < window_index[:, None]) | (
        (window_index[None, :] == window_index[:, None]) & earlier
    )
    place = jnp.sum(before, axis=1)
    slots = jnp.sum(
        jnp.where(place[None, :] == order[:, None], slot_index[None, :], 0), axis=1
    ).astype(jnp.int32)
    bounds = jnp.arange(windows + 1, dtype=jnp.int32)
    starts = jnp.sum(window_index[None, :] < bounds[:, None], axis=1).astype(jnp.int32)

    ahead, conjugate = complex_tables(window_cells)
    plane = (2, window_cells, window_cells)
    per_window = pl.BlockSpec((1, *plane), lambda number, *_: (number, 0, 0, 0))
    kept = jax.ShapeDtypeStruct((windows, *plane), jnp.bfloat16)
    flops = windows * 16 * window_cells**3
    far, phase = pl.pallas_call(
        functools.partial(forward_kernel, spots),
        grid=(windows,),
        out_shape=(kept, kept),
        in_specs=[whole(extended.shape), whole(plane), whole(ahead.shape), whole(ahead.shape)],
        out_specs=(per_window, per_window),
        cost_estimate=pl.CostEstimate(
            flops=flops, bytes_accessed=12 << 20, transcendentals=windows * window_cells**2
        ),
        name="forward",
    )(extended, probe_field, ahead, conjugate)

    gradient_sum, illumination = pl.pallas_call(
        functools.partial(backward_kernel, spots),
        out_shape=(
            jax.ShapeDtypeStruct((2, ext_rows, ext_cols), jnp.float32),
            jax.ShapeDtypeStruct((ext_rows, ext_cols), jnp.float32),
        ),
        grid_spec=pltpu.PrefetchScalarGridSpec(
            num_scalar_prefetch=2,
            grid=(windows,),
            in_specs=[
                per_window,
                per_window,
                pl.BlockSpec(
                    arrived.shape, lambda *_: (0, 0, 0), pipeline_mode=pl.Buffered(1)
                ),
                whole(plane),
                whole(ahead.shape),
                whole(ahead.shape),
            ],
            out_specs=(whole((2, ext_rows, ext_cols)), whole((ext_rows, ext_cols))),
            scratch_shapes=[pltpu.VMEM((window_cells, window_cells), jnp.float32)],
        ),
        cost_estimate=pl.CostEstimate(flops=flops, bytes_accessed=24 << 20, transcendentals=0),
        name="backward",
    )(slots, starts, far, phase, arrived, probe_field, ahead, conjugate)

    from_above = (
        from_behind(gradient_sum[:, tile_rows:, :].astype(jnp.bfloat16), "tx", 1).astype(
            jnp.float32
        ),
        from_behind(illumination[tile_rows:, :].astype(jnp.bfloat16), "tx", 1).astype(jnp.float32),
    )
    grad_top = gradient_sum[:, :tile_rows, :].at[:, :block_cells, :].add(from_above[0])
    light_top = illumination[:tile_rows, :].at[:block_cells, :].add(from_above[1])
    from_left = (
        from_behind(grad_top[:, :, tile_cols:].astype(jnp.bfloat16), "ty", 1).astype(jnp.float32),
        from_behind(light_top[:, tile_cols:].astype(jnp.bfloat16), "ty", 1).astype(jnp.float32),
    )
    grad_tile = grad_top[:, :, :tile_cols].at[:, :, :block_cells].add(from_left[0])
    light_tile = light_top[:, :tile_cols].at[:, :block_cells].add(from_left[1])
    updated = object_field - grad_tile / (light_tile + 1.0)
    for number in range(STEPS):
        padded = extended_2(updated, (("tx", 1), ("ty", 2)), 1)
        updated = smooth_pass(padded)
    return updated


def solution(mesh):
    in_specs = (
        P(None, "tx", "ty"),
        P(),
        P("tx", "ty", None),
        P(("tx", "ty"), None),
        P(("tx", "ty")),
    )
    out_specs = P(None, "tx", "ty")
    return jax.shard_map(local, mesh=mesh, in_specs=in_specs, out_specs=out_specs, check_vma=False)
```

time: 1410 us -> 324 us (0.23)
  matrix products: 359 us -> 0 us
  local copies, waits for them, and re-layouts: 294 us -> 7.69 us
  waiting for transfers between devices: 360 us -> 154 us
  starting transfers between devices: 237 us -> 81.3 us
  loops' own time: 69.8 us -> 0 us
  Pallas kernels: 0 us -> 34.3 us
  other arithmetic: 76.4 us -> 44.4 us
    dot_general x258 -> x0, matrix products: 359 us -> none  [the longest x128 183 us: right_product(): jnp.einsum('njk,kl->njl', values, table, preferred_element_type=jnp.float32)]
    all_to_all x2 -> x1, waiting for transfers between devices: 311 us -> 0.01 us  [local(): lax.all_to_all(amplitudes.astype(jnp.bfloat16), 'tx', split_axis=0, conca...]
    dynamic_update_slice x32 -> x0, local copies, waits for them, and re-layouts: 144 us -> none  [the longest x16 85.4 us: deposit_one(): lax.dynamic_update_slice(gradient_sum, region + own_grads[number], (ancho...]
    ppermute x6, starting transfers between devices: 158 us -> 20.7 us  [from_behind(): lax.ppermute(value, axis, [(source, source + steps) for source in range(i...]
    ppermute x6, waiting for transfers between devices: 34.9 us -> 141 us  [from_behind(): lax.ppermute(value, axis, [(source, source + steps) for source in range(i...]
    dynamic_slice x80 -> x0, local copies, waits for them, and re-layouts: 84 us -> none  [the longest x16 40.9 us: deposit_one(): own_grads[number]]
    another operation x3 -> x0, loops' own time: 69.8 us -> none  [the longest x1 59.1 us: local(): lax.fori_loop(0, positions_here, deposit_one, initial)]
    gather x48 -> x0, local copies, waits for them, and re-layouts: 44.9 us -> none
  transfers between devices with their start and end apart: 24 -> 23, of which waited for: 15 -> 13; matrix products, arithmetic and copies ran while one was open for 0% -> 3% of each run, Pallas kernels for 0% -> 5%
where the time goes in v1:
time: 324 us; the launch traced here: 323 us
  waiting for transfers between devices  154 us (48%)
  starting transfers between devices  81.3 us (25%)
  other arithmetic  44.4 us (14%)
  Pallas kernels  34.3 us (11%)
  local copies, waits for them, and re-layouts  7.69 us (2%)
    ppermute x6, waiting for transfers between devices, from_behind(): lax.ppermute(value, axis, [(source, source + steps) for source in range(i...  141 us
    ppermute x8, starting transfers between devices, extended_2(): after = lax.ppermute(initial, axis, down)  31.6 us
    ppermute x8, starting transfers between devices, extended_2(): before = lax.ppermute(last, axis, up)  22 us
    ppermute x6, starting transfers between devices, from_behind(): lax.ppermute(value, axis, [(source, source + steps) for source in range(i...  20.7 us
    pallas_call x1, Pallas kernels, local(): pl.pallas_call(functools.partial(backward_kernel, spots), out_shape=(jax....  18.8 us
    pallas_call x1, Pallas kernels, local(): pl.pallas_call(functools.partial(forward_kernel, spots), grid=(windows,),...  15.5 us
    add x4, other arithmetic, smooth_pass(): return center + TIME_STEP * flux_sum  15.1 us
    ppermute x8, waiting for transfers between devices, extended_2(): after = lax.ppermute(initial, axis, down)  13.5 us
  transfers between devices with their start and end apart: 23, of which 13 were waited for; matrix products, arithmetic and copies ran while one was open for 3% of the time, Pallas kernels for 5%

profile of v1, /device:TPU:7, one launch (start us, length us, event | category | flops | bytes accessed | tf_op | source)
XLA Modules:
  0.0 322.5 jit_solution(5357002680302349064)
XLA Ops:
  0.0 8.1 %convert_element_type.31 = bf16[48,256,256]{2,1,0:T(8,128)(2,1)} convert(f32[48,256,256]{2,1,0:T(8,128)} %param.17) | non-fusion elementwise | flops 3145728 | bytes 18874368 | tf_op jit(solution)/shard_map/convert_element_type | solution.py:151
  8.1 7.0 %all-to-all-start = ((bf16[48,256,256]{2,1,0:T(8,128)(2,1)}), bf16[48,256,256]{2,1,0:T(8,128)(2,1)}, u32[]{:S(2)}, u32[]{:S(2)}) async-start(bf16[48,256,256]{2,1,0:T(8,128)(2,1)} %convert_element_type.31), calls=%async_computation | async-start | bytes 12582912 | tf_op jit(solution)/shard_map/all_to_all | solution.py:150
  15.1 4.6 %collective-permute-start = (f32[2,128,512]{2,1,0:T(8,128)S(1)}, f32[2,128,512]{2,1,0:T(8,128)S(1)}, u32[]{:S(2)}, u32[]{:S(2)}) collective-permute-start(f32[2,128,512]{2,1,0:T(8,128)S(1)} %slice.372), channel_id=1, source_target_pairs={{8,0},{16,8},{24,16},{32,24},{40,32},{48,40},{56,48},{64,56},{72,6... | collective-permute-start | bytes 1572872 | tf_op jit(solution)/shard_map/ppermute | solution.py:22
  20.4 114.5 %collective-permute-done = f32[2,128,512]{2,1,0:T(8,128)S(1)} collective-permute-done((f32[2,128,512]{2,1,0:T(8,128)S(1)}, f32[2,128,512]{2,1,0:T(8,128)S(1)}, u32[]{:S(2)}, u32[]{:S(2)}) %collective-permute-start) | collective-permute-done | bytes 524320 | tf_op jit(solution)/shard_map/ppermute | solution.py:22
  135.1 3.7 %collective-permute-start.1 = (f32[2,640,128]{2,1,0:T(8,128)S(1)}, f32[2,640,128]{2,1,0:T(8,128)S(1)}, u32[]{:S(2)}, u32[]{:S(2)}) collective-permute-start(f32[2,640,128]{2,1,0:T(8,128)S(1)} %slice.450), channel_id=1, source_target_pairs={{1,0},{2,1},{3,2},{4,3},{5,4},{6,5},{7,6},{9,8},{10,9},{11,10},{12... | collective-permute-start | bytes 1966088 | tf_op jit(solution)/shard_map/ppermute | solution.py:22
  140.5 8.0 %collective-permute-done.1 = f32[2,640,128]{2,1,0:T(8,128)S(1)} collective-permute-done((f32[2,640,128]{2,1,0:T(8,128)S(1)}, f32[2,640,128]{2,1,0:T(8,128)S(1)}, u32[]{:S(2)}, u32[]{:S(2)}) %collective-permute-start.1) | collective-permute-done | bytes 655392 | tf_op jit(solution)/shard_map/ppermute | solution.py:22
  150.5 15.5 %forward.1 = (bf16[16,2,256,256]{3,2,1,0:T(8,128)(2,1)}, bf16[16,2,256,256]{3,2,1,0:T(8,128)(2,1)}) custom-call(f32[2,640,640]{2,1,0:T(8,128)} %pad_maximum_fusion.extended, f32[2,256,256]{2,1,0:T(8,128)} %probe.3, bf16[512,512]{1,0:T(8,128)(2,1)} %constant.129.clone.ahead, bf16[512,512]{1,0:T(8,128)(2,1)} %constant.130.clone.conjugate), custom_call_target="tpu_custom_call" | custom-call | flops 4294967296 | bytes 12582912 | tf_op jit(solution)/shard_map/forward/pallas_call | solution.py:182
  165.9 18.8 %backward.1 = (f32[2,640,640]{2,1,0:T(8,128)}, f32[640,640]{1,0:T(8,128)}) custom-call(s32[16]{0:T(128)} %select_reduce_fusion.slots, s32[17]{0:T(128)} %convert_reduce_fusion.starts, bf16[16,2,256,256]{3,2,1,0:T(8,128)(2,1)} %get-tuple-element.57.far, bf16[16,2,256,256]{3,2,1,0:T(8,128)(2,1)} %get-tuple-element.58.phase, ...), custom_call_target="tpu_custom_call" | custom-call | flops 4294967296 | bytes 25165824 | tf_op jit(solution)/shard_map/backward/pallas_call | solution.py:194
  189.3 6.2 %collective-permute-done.4 = bf16[128,640]{1,0:T(8,128)(2,1)S(1)} collective-permute-done((bf16[128,640]{1,0:T(8,128)(2,1)S(1)}, bf16[128,640]{1,0:T(8,128)(2,1)S(1)}, u32[]{:S(2)}, u32[]{:S(2)}) %collective-permute-start.4) | collective-permute-done | bytes 163872 | tf_op jit(solution)/shard_map/ppermute | solution.py:22
  196.5 3.9 %collective-permute-start.5 = (bf16[512,128]{1,0:T(8,128)(2,1)S(1)}, bf16[512,128]{1,0:T(8,128)(2,1)S(1)}, u32[]{:S(2)}, u32[]{:S(2)}) collective-permute-start(bf16[512,128]{1,0:T(8,128)(2,1)S(1)} %slice.706), channel_id=1, source_target_pairs={{0,1},{1,2},{2,3},{3,4},{4,5},{5,6},{6,7},{8,9},{9,10},{10,11},{11... | collective-permute-start | bytes 393224 | tf_op jit(solution)/shard_map/ppermute | solution.py:22
  204.1 8.8 %collective-permute-done.2 = bf16[2,128,640]{2,1,0:T(8,128)(2,1)S(1)} collective-permute-done((bf16[2,128,640]{2,1,0:T(8,128)(2,1)S(1)}, bf16[2,128,640]{2,1,0:T(8,128)(2,1)S(1)}, u32[]{:S(2)}, u32[]{:S(2)}) %collective-permute-start.2) | collective-permute-done | bytes 327712 | tf_op jit(solution)/shard_map/ppermute | solution.py:22
  213.0 4.6 %collective-permute-start.3 = (bf16[2,512,128]{2,1,0:T(8,128)(2,1)S(1)}, bf16[2,512,128]{2,1,0:T(8,128)(2,1)S(1)}, u32[]{:S(2)}, u32[]{:S(2)}) collective-permute-start(bf16[2,512,128]{2,1,0:T(8,128)(2,1)S(1)} %slice.704), channel_id=1, source_target_pairs={{0,1},{1,2},{2,3},{3,4},{4,5},{5,6},{6,7},{8,9},{9,10},{10,11},{11... | collective-permute-start | bytes 786440 | tf_op jit(solution)/shard_map/ppermute | solution.py:22
  218.1 2.9 collective-permute-done.3
  223.6 5.5 %collective-permute-start.7 = (f32[2,1,512]{2,1,0:T(1,128)S(1)}, f32[2,1,512]{2,1,0:T(1,128)S(1)}, u32[]{:S(2)}, u32[]{:S(2)}) collective-permute-start(f32[2,1,512]{2,1,0:T(1,128)S(1)} %get-tuple-element.92), channel_id=1, source_target_pairs={{8,0},{16,8},{24,16},{32,24},{40,32},{48,40},{56,48},{64,56},{72,6... | collective-permute-start | bytes 12296 | tf_op jit(solution)/shard_map/ppermute | solution.py:33
  230.3 5.5 %collective-permute-start.8 = (f32[2,514,1]{1,0,2:T(2,128)S(1)}, f32[2,514,1]{1,0,2:T(2,128)S(1)}, u32[]{:S(2)}, u32[]{:S(2)}) collective-permute-start(f32[2,514,1]{1,0,2:T(2,128)S(1)} %copy.24), channel_id=1, source_target_pairs={{0,1},{1,2},{2,3},{3,4},{4,5},{5,6},{6,7},{8,9},{9,10},{10,11},{11... | collective-permute-start | bytes 12344 | tf_op jit(solution)/shard_map/ppermute | solution.py:32
  238.2 2.8 collective-permute-done.9
  241.2 2.4 fusion.13
  244.6 3.5 %multiply_add_fusion.3 = f32[2,512,512]{2,1,0:T(8,128)S(1)} fusion(f32[2,512,512]{2,1,0:T(8,128)S(1)} %divide_subtract_fusion, f32[512,512]{1,0:T(8,128)S(1)} %get-tuple-element.93, f32[512,512]{1,0:T(8,128)S(1)} %get-tuple-element.94, f32[512,512]{1,0:T(8,128)S(1)} %get-tuple-element.95, f32[512,512]{1,0:T(8,128)S(1)} %get-tuple-element.96, ...), kind=kLoop, calls=%fused_computation.52 | loop fusion | flops 11010048 | bytes 8405024 | tf_op jit(solution)/shard_map/add | solution.py:137
  250.1 6.0 %collective-permute-start.11 = (f32[2,1,512]{2,1,0:T(1,128)S(1)}, f32[2,1,512]{2,1,0:T(1,128)S(1)}, u32[]{:S(2)}, u32[]{:S(2)}) collective-permute-start(f32[2,1,512]{2,1,0:T(1,128)S(1)} %get-tuple-element.90), channel_id=1, source_target_pairs={{8,0},{16,8},{24,16},{32,24},{40,32},{48,40},{56,48},{64,56},{72,6... | collective-permute-start | bytes 12296 | tf_op jit(solution)/shard_map/ppermute | solution.py:33
  257.4 2.9 collective-permute-start.12
  262.9 2.6 collective-permute-done.13
  265.7 2.4 fusion.9
  269.1 3.5 %multiply_add_fusion.2 = f32[2,512,512]{2,1,0:T(8,128)S(1)} fusion(f32[2,512,512]{2,1,0:T(8,128)S(1)} %copy-done.1, f32[512,512]{1,0:T(8,128)S(1)} %fusion.51, f32[512,512]{1,0:T(8,128)S(1)} %fusion.55, f32[512,512]{1,0:T(8,128)S(1)} %fusion.59, f32[512,512]{1,0:T(8,128)S(1)} %fusion.63, f32[2,1,512]{2,1,0:T(1,128)S(1)} %collective-permute-done.10, ...), kind=kLoop, calls=%fused_computation.51 | loop fusion | flops 11010048 | bytes 8405024 | tf_op jit(solution)/shard_map/add | solution.py:137
  274.6 6.0 %collective-permute-start.15 = (f32[2,1,512]{2,1,0:T(1,128)S(1)}, f32[2,1,512]{2,1,0:T(1,128)S(1)}, u32[]{:S(2)}, u32[]{:S(2)}) collective-permute-start(f32[2,1,512]{2,1,0:T(1,128)S(1)} %get-tuple-element.88), channel_id=1, source_target_pairs={{8,0},{16,8},{24,16},{32,24},{40,32},{48,40},{56,48},{64,56},{72,6... | collective-permute-start | bytes 12296 | tf_op jit(solution)/shard_map/ppermute | solution.py:33
  281.8 2.9 collective-permute-start.16
  287.2 2.8 collective-permute-done.17
  290.2 2.4 fusion.5
  293.6 3.5 %multiply_add_fusion.1 = f32[2,512,512]{2,1,0:T(8,128)S(1)} fusion(f32[2,512,512]{2,1,0:T(8,128)S(1)} %copy-done.3, f32[512,512]{1,0:T(8,128)S(1)} %fusion.35, f32[512,512]{1,0:T(8,128)S(1)} %fusion.39, f32[512,512]{1,0:T(8,128)S(1)} %fusion.43, f32[512,512]{1,0:T(8,128)S(1)} %fusion.47, f32[2,1,512]{2,1,0:T(1,128)S(1)} %collective-permute-done.14, ...), kind=kLoop, calls=%fused_computation.50 | loop fusion | flops 11010048 | bytes 8405024 | tf_op jit(solution)/shard_map/add | solution.py:137
  299.1 6.0 %collective-permute-start.19 = (f32[2,1,512]{2,1,0:T(1,128)S(1)}, f32[2,1,512]{2,1,0:T(1,128)S(1)}, u32[]{:S(2)}, u32[]{:S(2)}) collective-permute-start(f32[2,1,512]{2,1,0:T(1,128)S(1)} %get-tuple-element.86), channel_id=1, source_target_pairs={{8,0},{16,8},{24,16},{32,24},{40,32},{48,40},{56,48},{64,56},{72,6... | collective-permute-start | bytes 12296 | tf_op jit(solution)/shard_map/ppermute | solution.py:33
  306.3 2.9 collective-permute-start.20
  311.9 2.5 collective-permute-done.21
  318.0 4.5 %multiply_add_fusion = f32[2,512,512]{2,1,0:T(8,128)} fusion(f32[2,512,512]{2,1,0:T(8,128)S(1)} %copy-done.5, f32[512,512]{1,0:T(8,128)S(1)} %fusion.19, f32[512,512]{1,0:T(8,128)S(1)} %fusion.23, f32[512,512]{1,0:T(8,128)S(1)} %fusion.27, f32[512,512]{1,0:T(8,128)S(1)} %fusion.31, f32[2,1,512]{2,1,0:T(1,128)S(1)} %collective-permute-done.18, ...), kind=kLoop, calls=%fused_computation.49 | loop fusion | flops 11010048 | bytes 8405024 | tf_op jit(solution)/shard_map/add | solution.py:137
  (111 shorter events, 44.3 us)
Async XLA Ops:
  8.1 7.0 %copy-start.6 = (f32[2,512,512]{2,1,0:T(8,128)S(1)}, f32[2,512,512]{2,1,0:T(8,128)}, u32[]{:S(2)}) copy-start(f32[2,512,512]{2,1,0:T(8,128)} %param.15) | copy-start | bytes 6291460
  8.1 157.9 %all-to-all-start = ((bf16[48,256,256]{2,1,0:T(8,128)(2,1)}), bf16[48,256,256]{2,1,0:T(8,128)(2,1)}, u32[]{:S(2)}, u32[]{:S(2)}) async-start(bf16[48,256,256]{2,1,0:T(8,128)(2,1)} %convert_element_type.31), calls=%async_computation | async-start | bytes 12582912 | tf_op jit(solution)/shard_map/all_to_all | solution.py:150
  15.1 119.8 %collective-permute-start = (f32[2,128,512]{2,1,0:T(8,128)S(1)}, f32[2,128,512]{2,1,0:T(8,128)S(1)}, u32[]{:S(2)}, u32[]{:S(2)}) collective-permute-start(f32[2,128,512]{2,1,0:T(8,128)S(1)} %slice.372), channel_id=1, source_target_pairs={{8,0},{16,8},{24,16},{32,24},{40,32},{48,40},{56,48},{64,56},{72,6... | collective-permute-start | bytes 1572872 | tf_op jit(solution)/shard_map/ppermute | solution.py:22
  20.4 118.5 %copy-start.10 = (s32[16]{0:T(128)S(1)}, s32[16]{0:T(128)}, u32[]{:S(2)}) copy-start(s32[16]{0:T(128)} %param.19) | copy-start | bytes 196
  135.1 13.5 %collective-permute-start.1 = (f32[2,640,128]{2,1,0:T(8,128)S(1)}, f32[2,640,128]{2,1,0:T(8,128)S(1)}, u32[]{:S(2)}, u32[]{:S(2)}) collective-permute-start(f32[2,640,128]{2,1,0:T(8,128)S(1)} %slice.450), channel_id=1, source_target_pairs={{1,0},{2,1},{3,2},{4,3},{5,4},{6,5},{7,6},{9,8},{10,9},{11,10},{12... | collective-permute-start | bytes 1966088 | tf_op jit(solution)/shard_map/ppermute | solution.py:22
  184.8 15.7 %copy-start.8 = (f32[2,640,640]{2,1,0:T(8,128)S(1)}, f32[2,640,640]{2,1,0:T(8,128)}, u32[]{:S(2)}) copy-start(f32[2,640,640]{2,1,0:T(8,128)} %get-tuple-element.59) | copy-start | bytes 9830404
  185.9 9.6 %collective-permute-start.4 = (bf16[128,640]{1,0:T(8,128)(2,1)S(1)}, bf16[128,640]{1,0:T(8,128)(2,1)S(1)}, u32[]{:S(2)}, u32[]{:S(2)}) collective-permute-start(bf16[128,640]{1,0:T(8,128)(2,1)S(1)} %slice.705), channel_id=1, source_target_pairs={{0,8},{8,16},{16,24},{24,32},{32,40},{40,48},{48,56},{56,64},{64,7... | collective-permute-start | bytes 491528 | tf_op jit(solution)/shard_map/ppermute | solution.py:22
  196.5 6.8 %collective-permute-start.5 = (bf16[512,128]{1,0:T(8,128)(2,1)S(1)}, bf16[512,128]{1,0:T(8,128)(2,1)S(1)}, u32[]{:S(2)}, u32[]{:S(2)}) collective-permute-start(bf16[512,128]{1,0:T(8,128)(2,1)S(1)} %slice.706), channel_id=1, source_target_pairs={{0,1},{1,2},{2,3},{3,4},{4,5},{5,6},{6,7},{8,9},{9,10},{10,11},{11... | collective-permute-start | bytes 393224 | tf_op jit(solution)/shard_map/ppermute | solution.py:22
  200.5 12.4 %collective-permute-start.2 = (bf16[2,128,640]{2,1,0:T(8,128)(2,1)S(1)}, bf16[2,128,640]{2,1,0:T(8,128)(2,1)S(1)}, u32[]{:S(2)}, u32[]{:S(2)}) collective-permute-start(bf16[2,128,640]{2,1,0:T(8,128)(2,1)S(1)} %slice.703), channel_id=1, source_target_pairs={{0,8},{8,16},{16,24},{24,32},{32,40},{40,48},{48,56},{56,64},{64,7... | collective-permute-start | bytes 983048 | tf_op jit(solution)/shard_map/ppermute | solution.py:22
  213.0 8.0 %collective-permute-start.3 = (bf16[2,512,128]{2,1,0:T(8,128)(2,1)S(1)}, bf16[2,512,128]{2,1,0:T(8,128)(2,1)S(1)}, u32[]{:S(2)}, u32[]{:S(2)}) collective-permute-start(bf16[2,512,128]{2,1,0:T(8,128)(2,1)S(1)} %slice.704), channel_id=1, source_target_pairs={{0,1},{1,2},{2,3},{3,4},{4,5},{5,6},{6,7},{8,9},{9,10},{10,11},{11... | collective-permute-start | bytes 786440 | tf_op jit(solution)/shard_map/ppermute | solution.py:22
  221.7 7.4 %collective-permute-start.6 = (f32[2,1,512]{2,1,0:T(1,128)S(1)}, f32[2,1,512]{2,1,0:T(1,128)S(1)}, u32[]{:S(2)}, u32[]{:S(2)}) collective-permute-start(f32[2,1,512]{2,1,0:T(1,128)S(1)} %get-tuple-element.91), channel_id=1, source_target_pairs={{0,8},{8,16},{16,24},{24,32},{32,40},{40,48},{48,56},{56,64},{64,7... | collective-permute-start | bytes 12296 | tf_op jit(solution)/shard_map/ppermute | solution.py:32
  223.6 6.2 %collective-permute-start.7 = (f32[2,1,512]{2,1,0:T(1,128)S(1)}, f32[2,1,512]{2,1,0:T(1,128)S(1)}, u32[]{:S(2)}, u32[]{:S(2)}) collective-permute-start(f32[2,1,512]{2,1,0:T(1,128)S(1)} %get-tuple-element.92), channel_id=1, source_target_pairs={{8,0},{16,8},{24,16},{32,24},{40,32},{48,40},{56,48},{64,56},{72,6... | collective-permute-start | bytes 12296 | tf_op jit(solution)/shard_map/ppermute | solution.py:33
  230.3 7.7 %collective-permute-start.8 = (f32[2,514,1]{1,0,2:T(2,128)S(1)}, f32[2,514,1]{1,0,2:T(2,128)S(1)}, u32[]{:S(2)}, u32[]{:S(2)}) collective-permute-start(f32[2,514,1]{1,0,2:T(2,128)S(1)} %copy.24), channel_id=1, source_target_pairs={{0,1},{1,2},{2,3},{3,4},{4,5},{5,6},{6,7},{8,9},{9,10},{10,11},{11... | collective-permute-start | bytes 12344 | tf_op jit(solution)/shard_map/ppermute | solution.py:32
  236.0 4.9 %collective-permute-start.9 = (f32[2,514,1]{1,0,2:T(2,128)S(1)}, f32[2,514,1]{1,0,2:T(2,128)S(1)}, u32[]{:S(2)}, u32[]{:S(2)}) collective-permute-start(f32[2,514,1]{1,0,2:T(2,128)S(1)} %copy.26), channel_id=1, source_target_pairs={{1,0},{2,1},{3,2},{4,3},{5,4},{6,5},{7,6},{9,8},{10,9},{11,10},{12... | collective-permute-start | bytes 12344 | tf_op jit(solution)/shard_map/ppermute | solution.py:33
  248.2 8.7 %copy-start = (f32[2,512,512]{2,1,0:T(8,128)}, f32[2,512,512]{2,1,0:T(8,128)S(1)}, u32[]{:S(2)}) copy-start(f32[2,512,512]{2,1,0:T(8,128)S(1)} %multiply_add_fusion.3) | copy-start | bytes 6291460
  248.2 8.0 %collective-permute-start.10 = (f32[2,1,512]{2,1,0:T(1,128)S(1)}, f32[2,1,512]{2,1,0:T(1,128)S(1)}, u32[]{:S(2)}, u32[]{:S(2)}) collective-permute-start(f32[2,1,512]{2,1,0:T(1,128)S(1)} %get-tuple-element.89), channel_id=1, source_target_pairs={{0,8},{8,16},{16,24},{24,32},{32,40},{40,48},{48,56},{56,64},{64,7... | collective-permute-start | bytes 12296 | tf_op jit(solution)/shard_map/ppermute | solution.py:32
  250.1 6.8 %collective-permute-start.11 = (f32[2,1,512]{2,1,0:T(1,128)S(1)}, f32[2,1,512]{2,1,0:T(1,128)S(1)}, u32[]{:S(2)}, u32[]{:S(2)}) collective-permute-start(f32[2,1,512]{2,1,0:T(1,128)S(1)} %get-tuple-element.90), channel_id=1, source_target_pairs={{8,0},{16,8},{24,16},{32,24},{40,32},{48,40},{56,48},{64,56},{72,6... | collective-permute-start | bytes 12296 | tf_op jit(solution)/shard_map/ppermute | solution.py:33
  257.1 8.6 %copy-start.1 = (f32[2,512,512]{2,1,0:T(8,128)S(1)}, f32[2,512,512]{2,1,0:T(8,128)}, u32[]{:S(2)}) copy-start(f32[2,512,512]{2,1,0:T(8,128)} %copy-done) | copy-start | bytes 6291460
  257.4 5.3 %collective-permute-start.12 = (f32[2,514,1]{1,0,2:T(2,128)S(1)}, f32[2,514,1]{1,0,2:T(2,128)S(1)}, u32[]{:S(2)}, u32[]{:S(2)}) collective-permute-start(f32[2,514,1]{1,0,2:T(2,128)S(1)} %copy.28), channel_id=1, source_target_pairs={{0,1},{1,2},{2,3},{3,4},{4,5},{5,6},{6,7},{8,9},{9,10},{10,11},{11... | collective-permute-start | bytes 12344 | tf_op jit(solution)/shard_map/ppermute | solution.py:32
  260.5 4.9 %collective-permute-start.13 = (f32[2,514,1]{1,0,2:T(2,128)S(1)}, f32[2,514,1]{1,0,2:T(2,128)S(1)}, u32[]{:S(2)}, u32[]{:S(2)}) collective-permute-start(f32[2,514,1]{1,0,2:T(2,128)S(1)} %copy.30), channel_id=1, source_target_pairs={{1,0},{2,1},{3,2},{4,3},{5,4},{6,5},{7,6},{9,8},{10,9},{11,10},{12... | collective-permute-start | bytes 12344 | tf_op jit(solution)/shard_map/ppermute | solution.py:33
  272.6 8.7 %copy-start.2 = (f32[2,512,512]{2,1,0:T(8,128)}, f32[2,512,512]{2,1,0:T(8,128)S(1)}, u32[]{:S(2)}) copy-start(f32[2,512,512]{2,1,0:T(8,128)S(1)} %multiply_add_fusion.2) | copy-start | bytes 6291460
  272.7 8.0 %collective-permute-start.14 = (f32[2,1,512]{2,1,0:T(1,128)S(1)}, f32[2,1,512]{2,1,0:T(1,128)S(1)}, u32[]{:S(2)}, u32[]{:S(2)}) collective-permute-start(f32[2,1,512]{2,1,0:T(1,128)S(1)} %get-tuple-element.87), channel_id=1, source_target_pairs={{0,8},{8,16},{16,24},{24,32},{32,40},{40,48},{48,56},{56,64},{64,7... | collective-permute-start | bytes 12296 | tf_op jit(solution)/shard_map/ppermute | solution.py:32
  274.6 6.8 %collective-permute-start.15 = (f32[2,1,512]{2,1,0:T(1,128)S(1)}, f32[2,1,512]{2,1,0:T(1,128)S(1)}, u32[]{:S(2)}, u32[]{:S(2)}) collective-permute-start(f32[2,1,512]{2,1,0:T(1,128)S(1)} %get-tuple-element.88), channel_id=1, source_target_pairs={{8,0},{16,8},{24,16},{32,24},{40,32},{48,40},{56,48},{64,56},{72,6... | collective-permute-start | bytes 12296 | tf_op jit(solution)/shard_map/ppermute | solution.py:33
  281.6 8.6 %copy-start.3 = (f32[2,512,512]{2,1,0:T(8,128)S(1)}, f32[2,512,512]{2,1,0:T(8,128)}, u32[]{:S(2)}) copy-start(f32[2,512,512]{2,1,0:T(8,128)} %copy-done.2) | copy-start | bytes 6291460
  281.8 5.1 %collective-permute-start.16 = (f32[2,514,1]{1,0,2:T(2,128)S(1)}, f32[2,514,1]{1,0,2:T(2,128)S(1)}, u32[]{:S(2)}, u32[]{:S(2)}) collective-permute-start(f32[2,514,1]{1,0,2:T(2,128)S(1)} %copy.32), channel_id=1, source_target_pairs={{0,1},{1,2},{2,3},{3,4},{4,5},{5,6},{6,7},{8,9},{9,10},{10,11},{11... | collective-permute-start | bytes 12344 | tf_op jit(solution)/shard_map/ppermute | solution.py:32
  285.0 4.9 %collective-permute-start.17 = (f32[2,514,1]{1,0,2:T(2,128)S(1)}, f32[2,514,1]{1,0,2:T(2,128)S(1)}, u32[]{:S(2)}, u32[]{:S(2)}) collective-permute-start(f32[2,514,1]{1,0,2:T(2,128)S(1)} %copy.34), channel_id=1, source_target_pairs={{1,0},{2,1},{3,2},{4,3},{5,4},{6,5},{7,6},{9,8},{10,9},{11,10},{12... | collective-permute-start | bytes 12344 | tf_op jit(solution)/shard_map/ppermute | solution.py:33
  297.1 8.7 %copy-start.4 = (f32[2,512,512]{2,1,0:T(8,128)}, f32[2,512,512]{2,1,0:T(8,128)S(1)}, u32[]{:S(2)}) copy-start(f32[2,512,512]{2,1,0:T(8,128)S(1)} %multiply_add_fusion.1) | copy-start | bytes 6291460
  297.1 8.0 %collective-permute-start.18 = (f32[2,1,512]{2,1,0:T(1,128)S(1)}, f32[2,1,512]{2,1,0:T(1,128)S(1)}, u32[]{:S(2)}, u32[]{:S(2)}) collective-permute-start(f32[2,1,512]{2,1,0:T(1,128)S(1)} %get-tuple-element.85), channel_id=1, source_target_pairs={{0,8},{8,16},{16,24},{24,32},{32,40},{40,48},{48,56},{56,64},{64,7... | collective-permute-start | bytes 12296 | tf_op jit(solution)/shard_map/ppermute | solution.py:32
  299.1 6.8 %collective-permute-start.19 = (f32[2,1,512]{2,1,0:T(1,128)S(1)}, f32[2,1,512]{2,1,0:T(1,128)S(1)}, u32[]{:S(2)}, u32[]{:S(2)}) collective-permute-start(f32[2,1,512]{2,1,0:T(1,128)S(1)} %get-tuple-element.86), channel_id=1, source_target_pairs={{8,0},{16,8},{24,16},{32,24},{40,32},{48,40},{56,48},{64,56},{72,6... | collective-permute-start | bytes 12296 | tf_op jit(solution)/shard_map/ppermute | solution.py:33
  306.1 8.6 %copy-start.5 = (f32[2,512,512]{2,1,0:T(8,128)S(1)}, f32[2,512,512]{2,1,0:T(8,128)}, u32[]{:S(2)}) copy-start(f32[2,512,512]{2,1,0:T(8,128)} %copy-done.4) | copy-start | bytes 6291460
  306.3 5.3 %collective-permute-start.20 = (f32[2,514,1]{1,0,2:T(2,128)S(1)}, f32[2,514,1]{1,0,2:T(2,128)S(1)}, u32[]{:S(2)}, u32[]{:S(2)}) collective-permute-start(f32[2,514,1]{1,0,2:T(2,128)S(1)} %copy.36), channel_id=1, source_target_pairs={{0,1},{1,2},{2,3},{3,4},{4,5},{5,6},{6,7},{8,9},{9,10},{10,11},{11... | collective-permute-start | bytes 12344 | tf_op jit(solution)/shard_map/ppermute | solution.py:32
  309.5 4.9 %collective-permute-start.21 = (f32[2,514,1]{1,0,2:T(2,128)S(1)}, f32[2,514,1]{1,0,2:T(2,128)S(1)}, u32[]{:S(2)}, u32[]{:S(2)}) collective-permute-start(f32[2,514,1]{1,0,2:T(2,128)S(1)} %copy.38), channel_id=1, source_target_pairs={{1,0},{2,1},{3,2},{4,3},{5,4},{6,5},{7,6},{9,8},{10,9},{11,10},{12... | collective-permute-start | bytes 12344 | tf_op jit(solution)/shard_map/ppermute | solution.py:33
  (2 other events, 4.0 us)

commit v2 on v1

--- a/solution.py
+++ b/solution.py
@@ -20,19 +20,6 @@
     count = lax.axis_size(axis)
     initial, last = (max(0, -steps), min(count, count - steps))
     return lax.ppermute(value, axis, [(source, source + steps) for source in range(initial, last)])
-
-
-def extended_2(array, sides, width):
-    for axis, dim in sides:
-        peers, length = (lax.axis_size(axis), array.shape[dim])
-        up = [(i, (i + 1) % peers) for i in range(peers - 1)]
-        down = [(j, i) for i, j in up]
-        last = lax.slice_in_dim(array, length - width, length, axis=dim)
-        initial = lax.slice_in_dim(array, 0, width, axis=dim)
-        before = lax.ppermute(last, axis, up)
-        after = lax.ppermute(initial, axis, down)
-        array = jnp.concatenate([before, array, after], axis=dim)
-    return array
 
 
 def complex_tables(window_cells):
@@ -77,7 +64,7 @@
 
 
 def backward_kernel(
-    spots, slots, starts, far, phase, arrived, probe, ahead, conjugate, grads, light, measured
+    spots, slots, starts, far, phase, arrived, probe, ahead, conjugate, grads, measured
 ):
     cells = probe.shape[1]
     number = pl.program_id(0)
@@ -85,7 +72,6 @@
     @pl.when(number == 0)
     def _():
         grads[...] = jnp.zeros_like(grads)
-        light[...] = jnp.zeros_like(light)
 
     first, last = starts[number], starts[number + 1]
 
@@ -113,28 +99,242 @@
         view = (pl.ds(start_row, cells), pl.ds(start_col, cells))
         grads[(0, *view)] += probe_re * near_re + probe_im * near_im
         grads[(1, *view)] += probe_re * near_im - probe_im * near_re
-        light[view] += count * (probe_re * probe_re + probe_im * probe_im)
 
 
 def whole(shape):
     return pl.BlockSpec(shape, lambda *_: (0,) * len(shape))
 
 
-def smooth_pass(padded):
-    center = padded[:, 1:-1, 1:-1]
-    flux_sum = jnp.zeros_like(center)
-    for neighbour in (
-        padded[:, :-2, 1:-1],
-        padded[:, 2:, 1:-1],
-        padded[:, 1:-1, :-2],
-        padded[:, 1:-1, 2:],
-    ):
-        difference = neighbour - center
-        weight = 1.0 / (
-            1.0 + (difference[0] * difference[0] + difference[1] * difference[1]) / KAPPA_SQ
+LANES = 128
+RIM = 8
+MESH = pl.DeviceIdType.MESH
+ONWARD = ((1, 0), (0, 1), (1, 1))
+AROUND = ((-1, 0), (1, 0), (0, -1), (0, 1), (-1, -1), (-1, 1), (1, -1), (1, 1))
+
+
+def flux(difference):
+    weight = 1.0 / (
+        1.0 + (difference[0] * difference[0] + difference[1] * difference[1]) * (1.0 / KAPPA_SQ)
+    )
+    return weight[None] * difference
+
+
+def finish_kernel(
+    sizes, field, grads, probe, counts, out,
+    sent_down, sent_right, sent_corner, got_down, got_right, got_corner, got_counts,
+    inverse, column_rims, got_rows, got_columns, got_corners, first, second,
+    send_sem, recv_sem, rim_send_sem, rim_recv_sem,
+):
+    n_tx, n_ty = sizes
+    rows, cols = field.shape[1:]
+    block = probe.shape[1] // 2
+    spots = cols // block
+    row, col = lax.axis_index("tx"), lax.axis_index("ty")
+
+    def device(step):
+        return (lax.rem(row + step[0] + n_tx, n_tx), lax.rem(col + step[1] + n_ty, n_ty))
+
+    barrier = pltpu.get_barrier_semaphore()
+    for step in AROUND:
+        pl.semaphore_signal(barrier, inc=1, device_id=device(step), device_id_type=MESH)
+
+    sent_down[...] = grads[:, rows:, :cols].astype(jnp.bfloat16)
+    sent_right[...] = grads[:, :rows, cols:].astype(jnp.bfloat16)
+    sent_corner[...] = grads[:, rows:, cols:].astype(jnp.bfloat16)
+    pl.semaphore_wait(barrier, len(AROUND))
+
+    def send(source, target, sems, number, step):
+        return pltpu.make_async_remote_copy(
+            src_ref=source,
+            dst_ref=target,
+            send_sem=sems[0].at[number],
+            recv_sem=sems[1].at[number],
+            device_id=device(step),
+            device_id_type=MESH,
         )
-        flux_sum = flux_sum + weight * difference
-    return center + TIME_STEP * flux_sum
+
+    sums = (send_sem, recv_sem)
+    sum_copies = [
+        send(source, target, sums, number, ONWARD[number])
+        for number, (source, target) in enumerate(
+            ((sent_down, got_down), (sent_right, got_right), (sent_corner, got_corner))
+        )
+    ]
+    count_copies = [
+        send(counts, got_counts.at[number], sums, 3 + number, step)
+        for number, step in enumerate(ONWARD)
+    ]
+    for copy in count_copies + sum_copies:
+        copy.start()
+
+    has_above, has_left = row > 0, col > 0
+    has_below, has_right = row < n_tx - 1, col < n_ty - 1
+    above, left = has_above.astype(jnp.float32), has_left.astype(jnp.float32)
+    for copy in count_copies:
+        copy.wait()
+
+    def count_of(block_row, block_col):
+        number = block_row % spots * spots + block_col % spots
+        if block_row < 0 and block_col < 0:
+            return got_counts[2, number : number + 1, :] * (above * left)
+        if block_row < 0:
+            return got_counts[0, number : number + 1, :] * above
+        if block_col < 0:
+            return got_counts[1, number : number + 1, :] * left
+        return counts[number : number + 1, :]
+
+    for block_row in range(rows // block):
+        for block_col in range(spots):
+            light = jnp.ones((block, block), jnp.float32)
+            for down in range(2):
+                for right in range(2):
+                    part = (pl.ds(down * block, block), pl.ds(right * block, block))
+                    power = probe[(0, *part)] ** 2 + probe[(1, *part)] ** 2
+                    light += count_of(block_row - down, block_col - right) * power
+            inverse[pl.ds(block_row * block, block), pl.ds(block_col * block, block)] = 1.0 / light
+
+    for copy in sum_copies:
+        copy.wait()
+    for part in range(2):
+        grads[part, :block, :cols] += got_down[part].astype(jnp.float32) * above
+        grads[part, :rows, :block] += got_right[part].astype(jnp.float32) * left
+        grads[part, :block, :block] += got_corner[part].astype(jnp.float32) * (above * left)
+        updated = field[part] - grads[part, :rows, :cols] * inverse[...]
+        first[part, pl.ds(2 * RIM, rows), pl.ds(0, cols)] = updated
+        column_rims[0, part] = updated[:, :LANES].T[:RIM]
+        column_rims[1, part] = updated[:, cols - LANES :].T[LANES - RIM :]
+
+    rims = (rim_send_sem, rim_recv_sem)
+    top, bottom = pl.ds(2 * RIM, RIM), pl.ds(2 * RIM + rows - RIM, RIM)
+    west, east = pl.ds(0, LANES), pl.ds(cols - LANES, LANES)
+    sources = (
+        (first.at[:, top, pl.ds(0, cols)], got_rows.at[1]),
+        (first.at[:, bottom, pl.ds(0, cols)], got_rows.at[0]),
+        (column_rims.at[0], got_columns.at[1]),
+        (column_rims.at[1], got_columns.at[0]),
+        (first.at[:, top, west], got_corners.at[3]),
+        (first.at[:, top, east], got_corners.at[2]),
+        (first.at[:, bottom, west], got_corners.at[1]),
+        (first.at[:, bottom, east], got_corners.at[0]),
+    )
+    rim_copies = [
+        send(source, target, rims, number, AROUND[number])
+        for number, (source, target) in enumerate(sources)
+    ]
+    for copy in rim_copies:
+        copy.start()
+    for copy in rim_copies:
+        copy.wait()
+
+    lanes = lax.broadcasted_iota(jnp.int32, (RIM, LANES), 1)
+    on_right = lanes < jnp.where(has_right, RIM, 0)
+    on_left = lanes >= jnp.where(has_left, LANES - RIM, LANES)
+    zero = jnp.zeros((), jnp.float32)
+    extra = pl.ds(cols, LANES)
+    for part in range(2):
+        for number, place, exists in ((0, RIM, has_above), (1, 2 * RIM + rows, has_below)):
+            corner = jnp.where(
+                on_left, got_corners[2 * number, part],
+                jnp.where(on_right, got_corners[2 * number + 1, part], zero),
+            )
+            first[part, pl.ds(place, RIM), pl.ds(0, cols)] = jnp.where(
+                exists, got_rows[number, part], zero
+            )
+            first[part, pl.ds(place, RIM), extra] = jnp.where(exists, corner, zero)
+        sides = jnp.concatenate(
+            [
+                jnp.where(has_right, got_columns[1, part], zero),
+                jnp.zeros((LANES - 2 * RIM, rows), jnp.float32),
+                jnp.where(has_left, got_columns[0, part], zero),
+            ],
+            axis=0,
+        )
+        first[part, pl.ds(2 * RIM, rows), extra] = sides.T
+
+    wide = cols + LANES
+    every = lax.broadcasted_iota(jnp.int32, (RIM, wide), 1)
+    lane_kept = (every < jnp.where(has_right, cols + RIM, cols)) | (
+        every >= jnp.where(has_left, wide - RIM, wide)
+    )
+    sublane = lax.broadcasted_iota(jnp.int32, (2, RIM, wide), 1)
+    chunks = rows // RIM + 2
+
+    def smooth(source, store, start, stop):
+        def chunk(number, earlier):
+            place = pl.multiple_of((number + 1) * RIM, RIM)
+            center = source[:, pl.ds(place, RIM), :]
+            below = source[:, pl.ds(pl.multiple_of(place + RIM, RIM), RIM), :]
+            lower = jnp.where(
+                sublane == RIM - 1,
+                pltpu.roll(below, RIM - 1, axis=1),
+                pltpu.roll(center, RIM - 1, axis=1),
+            )
+            down = flux(lower - center)
+            up = jnp.where(
+                sublane == 0, pltpu.roll(earlier, 1, axis=1), pltpu.roll(down, 1, axis=1)
+            )
+            right = flux(pltpu.roll(center, wide - 1, axis=2) - center)
+            left_flux = pltpu.roll(right, 1, axis=2)
+            store(number, place, center + TIME_STEP * ((down - up) + (right - left_flux)))
+            return down
+
+        lax.fori_loop(start, stop, chunk, jnp.zeros((2, RIM, wide), jnp.float32))
+
+    def keep(target):
+        def store(number, place, value):
+            exists = jnp.where(
+                number == 0, has_above, jnp.where(number == chunks - 1, has_below, True)
+            )
+            kept = lane_kept & exists
+            target[:, pl.ds(place, RIM), :] = jnp.where(kept[None], value, zero)
+
+        return store
+
+    def give(number, place, value):
+        target = pl.multiple_of(place - 2 * RIM, RIM)
+        @pl.when(number > 0)
+        def _():
+            out[:, pl.ds(target, RIM), :] = value[:, :, :cols]
+
+    now, later = first, second
+    for _ in range(STEPS - 1):
+        smooth(now, keep(later), 0, chunks)
+        now, later = later, now
+    smooth(now, give, 0, chunks - 1)
+
+
+def finish(object_field, gradient_sum, probe_field, counts):
+    rows, cols = object_field.shape[1:]
+    block = probe_field.shape[1] // 2
+    sizes = (lax.axis_size("tx"), lax.axis_size("ty"))
+    tall, wide = rows + 4 * RIM, cols + LANES
+    strips = [(2, block, cols), (2, rows, block), (2, block, block)]
+    vmem = pl.BlockSpec(memory_space=pltpu.VMEM)
+    return pl.pallas_call(
+        functools.partial(finish_kernel, sizes),
+        out_shape=jax.ShapeDtypeStruct(object_field.shape, jnp.float32),
+        in_specs=[vmem] * 4,
+        out_specs=vmem,
+        scratch_shapes=[
+            *(pltpu.VMEM(strip, jnp.bfloat16) for strip in strips * 2),
+            pltpu.VMEM((3, *counts.shape), jnp.float32),
+            pltpu.VMEM((rows, cols), jnp.float32),
+            pltpu.VMEM((2, 2, RIM, rows), jnp.float32),
+            pltpu.VMEM((2, 2, RIM, cols), jnp.float32),
+            pltpu.VMEM((2, 2, RIM, rows), jnp.float32),
+            pltpu.VMEM((4, 2, RIM, LANES), jnp.float32),
+            pltpu.VMEM((2, tall, wide), jnp.float32),
+            pltpu.VMEM((2, tall, wide), jnp.float32),
+            pltpu.SemaphoreType.DMA((6,)),
+            pltpu.SemaphoreType.DMA((6,)),
+            pltpu.SemaphoreType.DMA((8,)),
+            pltpu.SemaphoreType.DMA((8,)),
+        ],
+        compiler_params=pltpu.CompilerParams(
+            collective_id=0, has_side_effects=True, vmem_limit_bytes=48 << 20
+        ),
+        name="finish",
+    )(object_field, gradient_sum, probe_field, counts)
 
 
 def local(object_field, probe_field, amplitudes, scan_blocks, owner_rows):
@@ -147,14 +347,12 @@
     windows = tile_rows // block_cells * spots
     ext_rows, ext_cols = tile_rows + block_cells, tile_cols + block_cells
 
-    arrived = lax.all_to_all(
-        amplitudes.astype(jnp.bfloat16), "tx", split_axis=0, concat_axis=0, tiled=True
-    )
-
     lower_rows = from_behind(object_field[:, :block_cells, :], "tx", -1)
     taller = jnp.concatenate([object_field, lower_rows], axis=1)
     right_cols = from_behind(taller[:, :, :block_cells], "ty", -1)
     extended = jnp.concatenate([taller, right_cols], axis=2)
+    outgoing, extended = lax.optimization_barrier((amplitudes.astype(jnp.bfloat16), extended))
+    arrived = lax.all_to_all(outgoing, "tx", split_axis=0, concat_axis=0, tiled=True)
 
     order = jnp.arange(positions_here, dtype=jnp.int32)
     earlier = order[None, :] < order[:, None]
@@ -191,12 +389,9 @@
         name="forward",
     )(extended, probe_field, ahead, conjugate)
 
-    gradient_sum, illumination = pl.pallas_call(
+    gradient_sum = pl.pallas_call(
         functools.partial(backward_kernel, spots),
-        out_shape=(
-            jax.ShapeDtypeStruct((2, ext_rows, ext_cols), jnp.float32),
-            jax.ShapeDtypeStruct((ext_rows, ext_cols), jnp.float32),
-        ),
+        out_shape=jax.ShapeDtypeStruct((2, ext_rows, ext_cols), jnp.float32),
         grid_spec=pltpu.PrefetchScalarGridSpec(
             num_scalar_prefetch=2,
             grid=(windows,),
@@ -210,32 +405,16 @@
                 whole(ahead.shape),
                 whole(ahead.shape),
             ],
-            out_specs=(whole((2, ext_rows, ext_cols)), whole((ext_rows, ext_cols))),
+            out_specs=whole((2, ext_rows, ext_cols)),
             scratch_shapes=[pltpu.VMEM((window_cells, window_cells), jnp.float32)],
         ),
         cost_estimate=pl.CostEstimate(flops=flops, bytes_accessed=24 << 20, transcendentals=0),
         name="backward",
     )(slots, starts, far, phase, arrived, probe_field, ahead, conjugate)
 
-    from_above = (
-        from_behind(gradient_sum[:, tile_rows:, :].astype(jnp.bfloat16), "tx", 1).astype(
-            jnp.float32
-        ),
-        from_behind(illumination[tile_rows:, :].astype(jnp.bfloat16), "tx", 1).astype(jnp.float32),
-    )
-    grad_top = gradient_sum[:, :tile_rows, :].at[:, :block_cells, :].add(from_above[0])
-    light_top = illumination[:tile_rows, :].at[:block_cells, :].add(from_above[1])
-    from_left = (
-        from_behind(grad_top[:, :, tile_cols:].astype(jnp.bfloat16), "ty", 1).astype(jnp.float32),
-        from_behind(light_top[:, tile_cols:].astype(jnp.bfloat16), "ty", 1).astype(jnp.float32),
-    )
-    grad_tile = grad_top[:, :, :tile_cols].at[:, :, :block_cells].add(from_left[0])
-    light_tile = light_top[:, :tile_cols].at[:, :block_cells].add(from_left[1])
-    updated = object_field - grad_tile / (light_tile + 1.0)
-    for number in range(STEPS):
-        padded = extended_2(updated, (("tx", 1), ("ty", 2)), 1)
-        updated = smooth_pass(padded)
-    return updated
+    counts = (starts[1:] - starts[:-1]).astype(jnp.float32)
+    counts = jnp.broadcast_to(counts[:, None], (windows, LANES))
+    return finish(object_field, gradient_sum, probe_field, counts)
 
 
 def solution(mesh):

time: 324 us -> 234 us (0.72)
  Pallas kernels: 34.3 us -> 117 us
  waiting for transfers between devices: 154 us -> 82.3 us
  starting transfers between devices: 81.3 us -> 16.5 us
  other arithmetic: 44.4 us -> 11.2 us
  local copies, waits for them, and re-layouts: 7.69 us -> 4.37 us
    ppermute x6 -> x2, waiting for transfers between devices: 141 us -> 10.5 us  [from_behind(): lax.ppermute(value, axis, [(source, source + steps) for source in range(i...]
    pallas_call x1 -> x2, Pallas kernels: 18.8 us -> 102 us  [the longest x1 82.6 us: finish(): pl.pallas_call(functools.partial(finish_kernel, sizes), out_shape=jax.Sha...]
    all_to_all x1, waiting for transfers between devices: 0.01 us -> 71.8 us  [local(): lax.all_to_all(outgoing, 'tx', split_axis=0, concat_axis=0, tiled=True)]
    ppermute x16 -> x0, starting transfers between devices: 53.7 us -> none  [the longest x8 31.6 us: extended_2(): after = lax.ppermute(initial, axis, down)]
    add x5 -> x0, other arithmetic: 15.2 us -> none  [the longest x4 15.1 us: smooth_pass(): return center + TIME_STEP * flux_sum]
    ppermute x16 -> x0, waiting for transfers between devices: 13.6 us -> none  [the longest x8 13.5 us: extended_2(): after = lax.ppermute(initial, axis, down)]
    ppermute x6 -> x2, starting transfers between devices: 20.7 us -> 8.35 us  [from_behind(): lax.ppermute(value, axis, [(source, source + steps) for source in range(i...]
    sub x5 -> x0, other arithmetic: 10.1 us -> none  [the longest x4 9.44 us: smooth_pass(): difference = neighbour - center]
  transfers between devices with their start and end apart: 23 -> 3, of which waited for: 13 -> 3; matrix products, arithmetic and copies ran while one was open for 3% -> 5% of each run, Pallas kernels for 5% -> 7%
where the time goes in v2:
time: 234 us; the launch traced here: 231 us
  Pallas kernels  117 us (50%)
  waiting for transfers between devices  82.3 us (35%)
  starting transfers between devices  16.5 us (7%)
  other arithmetic  11.2 us (5%)
  local copies, waits for them, and re-layouts  4.37 us (2%)
    pallas_call x1, Pallas kernels, finish(): pl.pallas_call(functools.partial(finish_kernel, sizes), out_shape=jax.Sha...  82.6 us
    all_to_all x1, waiting for transfers between devices, local(): lax.all_to_all(outgoing, 'tx', split_axis=0, concat_axis=0, tiled=True)  71.8 us
    pallas_call x1, Pallas kernels, local(): pl.pallas_call(functools.partial(backward_kernel, spots), out_shape=jax.S...  18.9 us
    pallas_call x1, Pallas kernels, local(): pl.pallas_call(functools.partial(forward_kernel, spots), grid=(windows,),...  15.5 us
    ppermute x2, waiting for transfers between devices, from_behind(): lax.ppermute(value, axis, [(source, source + steps) for source in range(i...  10.5 us
    ppermute x2, starting transfers between devices, from_behind(): lax.ppermute(value, axis, [(source, source + steps) for source in range(i...  8.35 us
    all_to_all x1, starting transfers between devices, local(): lax.all_to_all(outgoing, 'tx', split_axis=0, concat_axis=0, tiled=True)  8.13 us
    convert_element_type x1, other arithmetic, local(): amplitudes.astype(jnp.bfloat16)  8.11 us
  transfers between devices with their start and end apart: 3, of which 3 were waited for; matrix products, arithmetic and copies ran while one was open for 5% of the time, Pallas kernels for 7%

profile of v2, /device:TPU:7, one launch (start us, length us, event | category | flops | bytes accessed | tf_op | source)
XLA Modules:
  0.0 231.5 jit_solution(11265191298266533863)
XLA Ops:
  0.0 1.1 slice.20
  1.1 4.9 %collective-permute-start = (f32[2,128,512]{2,1,0:T(8,128)S(1)}, f32[2,128,512]{2,1,0:T(8,128)S(1)}, u32[]{:S(2)}, u32[]{:S(2)}) collective-permute-start(f32[2,128,512]{2,1,0:T(8,128)S(1)} %slice.20), channel_id=1, source_target_pairs={{8,0},{16,8},{24,16},{32,24},{40,32},{48,40},{56,48},{64,56},{72,6... | collective-permute-start | bytes 1572872 | tf_op jit(solution)/shard_map/ppermute | solution.py:22
  6.0 1.8 constant_dynamic-update-slice_fusion.1
  7.8 8.8 %collective-permute-done = f32[2,128,512]{2,1,0:T(8,128)S(1)} collective-permute-done((f32[2,128,512]{2,1,0:T(8,128)S(1)}, f32[2,128,512]{2,1,0:T(8,128)S(1)}, u32[]{:S(2)}, u32[]{:S(2)}) %collective-permute-start) | collective-permute-done | bytes 524320 | tf_op jit(solution)/shard_map/ppermute | solution.py:22
  16.6 0.1 slice.24
  16.7 3.4 %collective-permute-start.1 = (f32[2,640,128]{2,1,0:T(8,128)S(1)}, f32[2,640,128]{2,1,0:T(8,128)S(1)}, u32[]{:S(2)}, u32[]{:S(2)}) collective-permute-start(f32[2,640,128]{2,1,0:T(8,128)S(1)} %slice.24), channel_id=1, source_target_pairs={{1,0},{2,1},{3,2},{4,3},{5,4},{6,5},{7,6},{9,8},{10,9},{11,10},{12... | collective-permute-start | bytes 1966088 | tf_op jit(solution)/shard_map/ppermute | solution.py:22
  20.2 8.1 %convert_element_type.18 = bf16[48,256,256]{2,1,0:T(8,128)(2,1)} convert(f32[48,256,256]{2,1,0:T(8,128)} %param.9) | non-fusion elementwise | flops 3145728 | bytes 18874368 | tf_op jit(solution)/shard_map/convert_element_type | solution.py:354
  28.3 1.7 collective-permute-done.1
  29.9 1.9 pad_maximum_fusion.extended
  31.9 0.0 copy-start.2
  31.9 0.0 copy-start.4
  31.9 8.1 %all-to-all-start = ((bf16[48,256,256]{2,1,0:T(8,128)(2,1)}), bf16[48,256,256]{2,1,0:T(8,128)(2,1)}, u32[]{:S(2)}, u32[]{:S(2)}) async-start(bf16[48,256,256]{2,1,0:T(8,128)(2,1)} %convert_element_type.18), calls=%async_computation | async-start | bytes 12582912 | tf_op jit(solution)/shard_map/all_to_all | solution.py:355
  40.0 0.0 copy-done.2
  40.0 0.2 convert_reduce_fusion.2
  40.2 0.0 copy-done.4
  40.2 0.2 convert_reduce_fusion.1
  40.4 0.6 select_reduce_fusion.slots
  41.0 0.1 convert_reduce_fusion.starts
  41.1 0.0 copy-start.3
  41.1 0.1 subtract_convert_fusion
  41.2 15.5 %forward.1 = (bf16[16,2,256,256]{3,2,1,0:T(8,128)(2,1)}, bf16[16,2,256,256]{3,2,1,0:T(8,128)(2,1)}) custom-call(f32[2,640,640]{2,1,0:T(8,128)} %pad_maximum_fusion.extended, f32[2,256,256]{2,1,0:T(8,128)} %probe.5, bf16[512,512]{1,0:T(8,128)(2,1)} %constant.20.clone.ahead, bf16[512,512]{1,0:T(8,128)(2,1)} %constant.21.clone.conjugate), custom_call_target="tpu_custom_call" | custom-call | flops 4294967296 | bytes 12582912 | tf_op jit(solution)/shard_map/forward/pallas_call | solution.py:380
  56.7 0.0 copy-done.3
  56.7 71.8 %all-to-all-done.arrived = bf16[48,256,256]{2,1,0:T(8,128)(2,1)} async-done(((bf16[48,256,256]{2,1,0:T(8,128)(2,1)}), bf16[48,256,256]{2,1,0:T(8,128)(2,1)}, u32[]{:S(2)}, u32[]{:S(2)}) %all-to-all-start) | async-done | bytes 6291488 | tf_op jit(solution)/shard_map/all_to_all | solution.py:355
  128.5 0.0 copy-start
  128.5 0.0 copy-start.1
  128.5 18.9 %backward.1.grads = f32[2,640,640]{2,1,0:T(8,128)} custom-call(s32[16]{0:T(128)} %select_reduce_fusion.slots, s32[17]{0:T(128)} %copy-done.3, bf16[16,2,256,256]{3,2,1,0:T(8,128)(2,1)} %get-tuple-element.10.far, bf16[16,2,256,256]{3,2,1,0:T(8,128)(2,1)} %get-tuple-element.11.phase, bf16[48,256,256]{2,1,0:T(8,128)(2,1)} %all-to-all-done.arrived, ...), custom_call_target="tpu_custom_call" | custom-call | flops 4294967296 | bytes 25165824 | tf_op jit(solution)/shard_map/backward/pallas_call | solution.py:392
  147.5 0.1 broadcast_in_dim.12.counts
  147.5 0.0 copy-done
  147.5 0.0 copy-done.1
  147.5 82.6 %finish.1 = f32[2,512,512]{2,1,0:T(8,128)S(1)} custom-call(f32[2,512,512]{2,1,0:T(8,128)S(1)} %copy-done, f32[2,640,640]{2,1,0:T(8,128)} %backward.1.grads, f32[2,256,256]{2,1,0:T(8,128)S(1)} %copy-done.1, f32[16,128]{1,0:T(8,128)S(1)} %broadcast_in_dim.12.counts), custom_call_target="tpu_custom_call" | custom-call | tf_op jit(solution)/shard_map/finish/pallas_call | solution.py:313
  230.1 1.3 copy.10
  (3 shorter events, 0.0 us)
Async XLA Ops:
  1.1 15.5 %collective-permute-start = (f32[2,128,512]{2,1,0:T(8,128)S(1)}, f32[2,128,512]{2,1,0:T(8,128)S(1)}, u32[]{:S(2)}, u32[]{:S(2)}) collective-permute-start(f32[2,128,512]{2,1,0:T(8,128)S(1)} %slice.20), channel_id=1, source_target_pairs={{8,0},{16,8},{24,16},{32,24},{40,32},{48,40},{56,48},{64,56},{72,6... | collective-permute-start | bytes 1572872 | tf_op jit(solution)/shard_map/ppermute | solution.py:22
  16.7 13.2 %collective-permute-start.1 = (f32[2,640,128]{2,1,0:T(8,128)S(1)}, f32[2,640,128]{2,1,0:T(8,128)S(1)}, u32[]{:S(2)}, u32[]{:S(2)}) collective-permute-start(f32[2,640,128]{2,1,0:T(8,128)S(1)} %slice.24), channel_id=1, source_target_pairs={{1,0},{2,1},{3,2},{4,3},{5,4},{6,5},{7,6},{9,8},{10,9},{11,10},{12... | collective-permute-start | bytes 1966088 | tf_op jit(solution)/shard_map/ppermute | solution.py:22
  31.9 8.1 %copy-start.2 = (s32[16,2]{0,1:T(2,128)S(1)}, s32[16,2]{0,1:T(2,128)}, u32[]{:S(2)}) copy-start(s32[16,2]{0,1:T(2,128)} %param.10) | copy-start | bytes 388
  31.9 8.3 %copy-start.4 = (s32[16]{0:T(128)S(1)}, s32[16]{0:T(128)}, u32[]{:S(2)}) copy-start(s32[16]{0:T(128)} %param.11) | copy-start | bytes 196
  31.9 96.7 %all-to-all-start = ((bf16[48,256,256]{2,1,0:T(8,128)(2,1)}), bf16[48,256,256]{2,1,0:T(8,128)(2,1)}, u32[]{:S(2)}, u32[]{:S(2)}) async-start(bf16[48,256,256]{2,1,0:T(8,128)(2,1)} %convert_element_type.18), calls=%async_computation | async-start | bytes 12582912 | tf_op jit(solution)/shard_map/all_to_all | solution.py:355
  41.1 15.6 %copy-start.3 = (s32[17]{0:T(128)}, s32[17]{0:T(128)S(1)}, u32[]{:S(2)}) copy-start(s32[17]{0:T(128)S(1)} %convert_reduce_fusion.starts) | copy-start | bytes 208
  128.5 19.0 %copy-start = (f32[2,512,512]{2,1,0:T(8,128)S(1)}, f32[2,512,512]{2,1,0:T(8,128)}, u32[]{:S(2)}) copy-start(f32[2,512,512]{2,1,0:T(8,128)} %field.1) | copy-start | bytes 6291460
  128.5 19.0 %copy-start.1 = (f32[2,256,256]{2,1,0:T(8,128)S(1)}, f32[2,256,256]{2,1,0:T(8,128)}, u32[]{:S(2)}) copy-start(f32[2,256,256]{2,1,0:T(8,128)} %probe.5) | copy-start | bytes 1572868

commit v3 on v2

--- a/solution.py
+++ b/solution.py
@@ -14,12 +14,6 @@
 KAPPA_SQ = 1.0
 TIME_STEP = 0.2
 AMPLITUDE_FLOOR = 0.5
-
-
-def from_behind(value, axis, steps):
-    count = lax.axis_size(axis)
-    initial, last = (max(0, -steps), min(count, count - steps))
-    return lax.ppermute(value, axis, [(source, source + steps) for source in range(initial, last)])
 
 
 def complex_tables(window_cells):
@@ -35,74 +29,6 @@
 
 def matmul(first, second):
     return jnp.dot(first, second, preferred_element_type=jnp.float32)
-
-
-def corner_of(number, spots, cells):
-    start_row = pl.multiple_of(number // spots * cells, cells)
-    start_col = pl.multiple_of(number % spots * cells, cells)
-    return start_row, start_col
-
-
-def forward_kernel(spots, extended, probe, ahead, conjugate, far_out, phase_out):
-    cells = probe.shape[1]
-    start_row, start_col = corner_of(pl.program_id(0), spots, cells // 2)
-    view = (pl.ds(start_row, cells), pl.ds(start_col, cells))
-    window_re, window_im = extended[(0, *view)], extended[(1, *view)]
-    probe_re, probe_im = probe[0], probe[1]
-    wave_re = (probe_re * window_re - probe_im * window_im).astype(jnp.bfloat16)
-    wave_im = (probe_re * window_im + probe_im * window_re).astype(jnp.bfloat16)
-    half = matmul(ahead[...], jnp.concatenate([wave_re, wave_im], axis=0)).astype(jnp.bfloat16)
-    far = matmul(jnp.concatenate([half[:cells], half[cells:]], axis=1), conjugate[...])
-    far_re, far_im = far[:, :cells], far[:, cells:]
-    inverse = jnp.minimum(
-        lax.rsqrt(far_re * far_re + far_im * far_im), 1.0 / AMPLITUDE_FLOOR
-    )
-    far_out[0, 0] = far_re.astype(jnp.bfloat16)
-    far_out[0, 1] = far_im.astype(jnp.bfloat16)
-    phase_out[0, 0] = (far_re * inverse).astype(jnp.bfloat16)
-    phase_out[0, 1] = (far_im * inverse).astype(jnp.bfloat16)
-
-
-def backward_kernel(
-    spots, slots, starts, far, phase, arrived, probe, ahead, conjugate, grads, measured
-):
-    cells = probe.shape[1]
-    number = pl.program_id(0)
-
-    @pl.when(number == 0)
-    def _():
-        grads[...] = jnp.zeros_like(grads)
-
-    first, last = starts[number], starts[number + 1]
-
-    @pl.when(last > first)
-    def _():
-        measured[...] = arrived[slots[first]].astype(jnp.float32)
-
-        def add_one(index, carry):
-            measured[...] += arrived[slots[index]].astype(jnp.float32)
-            return carry
-
-        lax.fori_loop(first + 1, last, add_one, 0)
-        count = (last - first).astype(jnp.float32)
-        total = measured[...]
-        residual = [
-            (far[0, part].astype(jnp.float32) * count
-             - phase[0, part].astype(jnp.float32) * total).astype(jnp.bfloat16)
-            for part in range(2)
-        ]
-        back = matmul(conjugate[...], jnp.concatenate(residual, axis=0)).astype(jnp.bfloat16)
-        near = matmul(jnp.concatenate([back[:cells], back[cells:]], axis=1), ahead[...])
-        near_re, near_im = near[:, :cells], near[:, cells:]
-        probe_re, probe_im = probe[0], probe[1]
-        start_row, start_col = corner_of(number, spots, cells // 2)
-        view = (pl.ds(start_row, cells), pl.ds(start_col, cells))
-        grads[(0, *view)] += probe_re * near_re + probe_im * near_im
-        grads[(1, *view)] += probe_re * near_im - probe_im * near_re
-
-
-def whole(shape):
-    return pl.BlockSpec(shape, lambda *_: (0,) * len(shape))
 
 
 LANES = 128
@@ -337,6 +263,343 @@
     )(object_field, gradient_sum, probe_field, counts)
 
 
+SIDE = 4
+STAGES = 4
+TAKEN = tuple(
+    sorted(
+        ((dx, dy) for dx in range(SIDE) for dy in range(SIDE)),
+        key=lambda step: (step == (0, 0), 2 not in step, 0 in step),
+    )
+)
+NEARBY = ((1, 0), (-1, 0), (0, 1), (0, -1), (1, 1), (-1, -1))
+
+
+def gather_kernel(
+    sizes, slots, same, ends, counts, field, amplitudes, probe, ahead, conjugate, grads,
+    extended, sent_rows, got_rows, staged, sent, arrived, held, passed, passed_again,
+    far, phase, sums, stage_sem, field_sem, own_sem, halo_send, halo_recv, send_sem, recv_sem,
+):
+    n_tx, n_ty = sizes
+    cells = probe.shape[1]
+    block = cells // 2
+    rows, cols = extended.shape[1] - block, extended.shape[2] - block
+    spots = cols // block
+    windows = rows // block * spots
+    row, col = lax.axis_index("tx"), lax.axis_index("ty")
+    place = (row // SIDE, lax.rem(row, SIDE))
+
+    def around(step):
+        return (lax.rem(row + step[0] + n_tx, n_tx), lax.rem(col + step[1] + n_ty, n_ty))
+
+    def owner_at(half, first, second):
+        first, second = lax.rem(first + SIDE, SIDE), lax.rem(second + SIDE, SIDE)
+        return first * SIDE + second if half == 0 else second * SIDE + first
+
+    def load(number):
+        dx, dy = TAKEN[number]
+        home = owner_at(0, place[0] + dx, place[1] + dy)
+        slot = number % STAGES
+        return pltpu.make_async_copy(
+            amplitudes.at[home], staged.at[slot], stage_sem.at[slot]
+        )
+
+    take_field = pltpu.make_async_copy(
+        field, extended.at[:, pl.ds(0, rows), pl.ds(0, cols)], field_sem
+    )
+    take_field.start()
+    for number in range(STAGES):
+        load(number).start()
+
+    barrier = pltpu.get_barrier_semaphore()
+    partners = [around(step) for step in NEARBY] + [
+        (owner_at(half, place[half] + step, place[1 - half]), col)
+        for half in range(2)
+        for step in (1, -1)
+    ]
+    for partner in partners:
+        pl.semaphore_signal(barrier, inc=1, device_id=partner, device_id_type=MESH)
+
+    def remote(source, target, sems, partner):
+        return pltpu.make_async_remote_copy(
+            src_ref=source,
+            dst_ref=target,
+            send_sem=sems[0],
+            recv_sem=sems[1],
+            device_id=partner,
+            device_id_type=MESH,
+        )
+
+    def piece(half, kind, first, second):
+        a, b = place[half], place[1 - half]
+        lines = pl.ds(half * block, block)
+        ring = 0 if kind < 4 else 1
+        number = kind * SIDE + (second if ring == 0 else first)
+        sems = (send_sem.at[half, number], recv_sem.at[half, number])
+        if ring == 0:
+            step = 1 if kind == 0 or (kind > 1 and second < 2) else -1
+            partner = owner_at(half, a + step, b)
+            if kind == 3:
+                source, owner = passed.at[half, second], owner_at(half, a - step, b)
+            else:
+                offset = (1, -1, 2)[kind]
+                source = sent.at[owner_at(half, a + offset, b + second), :, lines]
+                owner = row
+            if kind == 2:
+                target = passed.at[half, second]
+            elif second == 0:
+                target = arrived.at[owner, :, lines]
+            else:
+                target = held.at[half, (0, 2, 2, 1)[kind], second - 1]
+        else:
+            step = 1 if kind == 4 or (kind > 5 and first < 2) else -1
+            partner = owner_at(half, a, b + step)
+            offset = (1, 3, 2)[kind - 4] if kind < 7 else 0
+            if kind == 7:
+                source = passed_again.at[half, first]
+                owner = owner_at(half, a - first, b - step)
+            else:
+                source = (
+                    sent.at[owner_at(half, a, b + offset), :, lines]
+                    if first == 0
+                    else held.at[half, first - 1, offset - 1]
+                )
+                owner = owner_at(half, a - first, b)
+            target = (
+                passed_again.at[half, first] if kind == 6 else arrived.at[owner, :, lines]
+            )
+        return remote(source, target, sems, (partner, col))
+
+    take_field.wait()
+    sent_rows[...] = extended[:, :block, :cols].astype(jnp.bfloat16)
+    pl.semaphore_wait(barrier, len(partners))
+
+    corner = (pl.ds(rows, block), pl.ds(cols, block))
+    halos = [
+        remote(sent_rows, got_rows, (halo_send.at[0], halo_recv.at[0]), around((-1, 0))),
+        remote(
+            extended.at[:, pl.ds(0, rows), pl.ds(0, block)],
+            extended.at[:, pl.ds(0, rows), pl.ds(cols, block)],
+            (halo_send.at[1], halo_recv.at[1]), around((0, -1)),
+        ),
+        remote(
+            extended.at[:, pl.ds(0, block), pl.ds(0, block)],
+            extended.at[(slice(None), *corner)],
+            (halo_send.at[2], halo_recv.at[2]), around((-1, -1)),
+        ),
+    ]
+
+    for number, (dx, dy) in enumerate(TAKEN):
+        slot = number % STAGES
+        home = owner_at(0, place[0] + dx, place[1] + dy)
+        load(number).wait()
+
+        def cast(index, carry):
+            sent[home, index] = staged[slot, index].astype(jnp.bfloat16)
+            return carry
+
+        lax.fori_loop(0, sent.shape[1], cast, 0)
+        if number + STAGES < len(TAKEN):
+            load(number + STAGES).start()
+        for half, (first, second) in enumerate(((dx, dy), (dy, dx))):
+            if first:
+                piece(half, (0, 2, 1)[first - 1], None, second).start()
+        if number == 6:
+            for copy in halos:
+                copy.start()
+
+    own = pltpu.make_async_copy(sent.at[row], arrived.at[row], own_sem)
+    own.start()
+
+    def forward(number):
+        start_row = pl.multiple_of(number // spots * block, block)
+        start_col = pl.multiple_of(lax.rem(number, spots) * block, block)
+        view = (pl.ds(start_row, cells), pl.ds(start_col, cells))
+        window_re, window_im = extended[(0, *view)], extended[(1, *view)]
+        probe_re, probe_im = probe[0], probe[1]
+        wave_re = (probe_re * window_re - probe_im * window_im).astype(jnp.bfloat16)
+        wave_im = (probe_re * window_im + probe_im * window_re).astype(jnp.bfloat16)
+        half = matmul(ahead[...], jnp.concatenate([wave_re, wave_im], axis=0)).astype(
+            jnp.bfloat16
+        )
+        waves = matmul(jnp.concatenate([half[:cells], half[cells:]], axis=1), conjugate[...])
+        far_re, far_im = waves[:, :cells], waves[:, cells:]
+        inverse = jnp.minimum(
+            lax.rsqrt(far_re * far_re + far_im * far_im), 1.0 / AMPLITUDE_FLOOR
+        )
+        far[number, 0] = far_re.astype(jnp.bfloat16)
+        far[number, 1] = far_im.astype(jnp.bfloat16)
+        phase[number, 0] = (far_re * inverse).astype(jnp.bfloat16)
+        phase[number, 1] = (far_im * inverse).astype(jnp.bfloat16)
+
+    def relay_first():
+        for second in range(SIDE):
+            for half in range(2):
+                piece(half, 2, None, second).wait_recv()
+                piece(half, 3, None, second).start()
+        for kind in (6, 4, 5):
+            for half in range(2):
+                piece(half, kind, 0, None).start()
+
+    def turn(first, second):
+        arrival = (0, 3, 1)[first - 1]
+        kind = {1: 4, 2: 6, 3: 5}[second]
+        for half in range(2):
+            piece(half, arrival, None, second).wait_recv()
+            piece(half, kind, first, None).start()
+
+    def relay_second(first):
+        for half in range(2):
+            piece(half, 6, first, None).wait_recv()
+            piece(half, 7, first, None).start()
+
+    def take_halos():
+        for copy in halos:
+            copy.wait()
+
+        for part in range(2):
+            extended[part, pl.ds(rows, block), pl.ds(0, cols)] = jnp.where(
+                row < n_tx - 1, got_rows[part].astype(jnp.float32), 0.0
+            )
+
+        @pl.when(col == n_ty - 1)
+        def _():
+            extended[:, :, pl.ds(cols, block)] = jnp.zeros_like(extended[:, :, cols:])
+
+        @pl.when(row == n_tx - 1)
+        def _():
+            extended[(slice(None), *corner)] = jnp.zeros((2, block, block), jnp.float32)
+
+    inner = spots - 1
+    steps = {
+        3: [relay_first],
+        5: [functools.partial(turn, 1, 2)],
+        7: [functools.partial(turn, 3, 2), take_halos],
+        9: [functools.partial(turn, 1, 1)],
+        11: [functools.partial(turn, 3, 1)],
+        13: [functools.partial(turn, 1, 3)],
+        14: [functools.partial(turn, 3, 3)],
+    }
+
+    def forward_step(index, carry):
+        edge = index - inner * inner
+        inside = index < inner * inner
+        at_row = jnp.where(inside, index // inner, jnp.where(edge < spots, inner, edge - spots))
+        at_col = jnp.where(inside, lax.rem(index, inner), jnp.where(edge < spots, edge, inner))
+        forward(at_row * spots + at_col)
+        for when, work in steps.items():
+
+            @pl.when(index == when)
+            def _(work=work):
+                for one in work:
+                    one()
+
+        return carry
+
+    lax.fori_loop(0, windows, forward_step, 0)
+    for second in (2, 1, 3):
+        turn(2, second)
+    grads[...] = jnp.zeros_like(grads)
+    for first in (0, 1, 3, 2):
+        relay_second(first)
+
+    own.wait()
+    for half in range(2):
+        for kind in (0, 1, 3):
+            piece(half, kind, None, 0).wait_recv()
+        for kind in (4, 5, 7):
+            for first in range(SIDE):
+                piece(half, kind, first, None).wait_recv()
+
+    def add_up(index, carry):
+        slot = slots[index]
+        plane = arrived[slot // arrived.shape[1], lax.rem(slot, arrived.shape[1])]
+        before = jnp.where(same[index] > 0, sums[jnp.maximum(index - 1, 0)], 0.0)
+        sums[index] = before + plane.astype(jnp.float32)
+        return carry
+
+    lax.fori_loop(0, sums.shape[0], add_up, 0)
+
+    def backward(number, carry):
+        count = counts[number]
+        total = sums[ends[number]] * jnp.minimum(count, 1.0)
+        residual = [
+            (
+                far[number, part].astype(jnp.float32) * count
+                - phase[number, part].astype(jnp.float32) * total
+            ).astype(jnp.bfloat16)
+            for part in range(2)
+        ]
+        back = matmul(conjugate[...], jnp.concatenate(residual, axis=0)).astype(jnp.bfloat16)
+        near = matmul(jnp.concatenate([back[:cells], back[cells:]], axis=1), ahead[...])
+        near_re, near_im = near[:, :cells], near[:, cells:]
+        probe_re, probe_im = probe[0], probe[1]
+        start_row = pl.multiple_of(number // spots * block, block)
+        start_col = pl.multiple_of(lax.rem(number, spots) * block, block)
+        view = (pl.ds(start_row, cells), pl.ds(start_col, cells))
+        grads[(0, *view)] += probe_re * near_re + probe_im * near_im
+        grads[(1, *view)] += probe_re * near_im - probe_im * near_re
+        return carry
+
+    lax.fori_loop(0, windows, backward, 0)
+    for half in range(2):
+        for kind in range(4):
+            for second in range(SIDE):
+                piece(half, kind, None, second).wait_send()
+        for kind in range(4, 8):
+            for first in range(SIDE):
+                piece(half, kind, first, None).wait_send()
+
+
+def gather(object_field, probe_field, amplitudes, tables, scalars):
+    rows, cols = object_field.shape[1:]
+    cells = probe_field.shape[1]
+    block = cells // 2
+    windows = rows // block * (cols // block)
+    groups = lax.axis_size("tx")
+    slots = amplitudes.shape[0] // groups
+    sizes = (groups, lax.axis_size("ty"))
+    assert groups == SIDE * SIDE
+    vmem = pl.BlockSpec(memory_space=pltpu.VMEM)
+    smem = pl.BlockSpec(memory_space=pltpu.SMEM)
+    anywhere = pl.BlockSpec(memory_space=pl.ANY)
+    narrow, wide = jnp.bfloat16, jnp.float32
+    own = (groups, slots, cells, cells)
+    part = (slots, block, cells)
+    return pl.pallas_call(
+        functools.partial(gather_kernel, sizes),
+        out_shape=jax.ShapeDtypeStruct((2, rows + block, cols + block), wide),
+        in_specs=[smem] * 4 + [anywhere] * 2 + [vmem] * 3,
+        out_specs=vmem,
+        scratch_shapes=[
+            pltpu.VMEM((2, rows + block, cols + block), wide),
+            pltpu.VMEM((2, block, cols), narrow),
+            pltpu.VMEM((2, block, cols), narrow),
+            pltpu.VMEM((STAGES, slots, cells, cells), wide),
+            pltpu.VMEM(own, narrow),
+            pltpu.VMEM(own, narrow),
+            pltpu.VMEM((2, SIDE - 1, SIDE - 1, *part), narrow),
+            pltpu.VMEM((2, SIDE, *part), narrow),
+            pltpu.VMEM((2, SIDE, *part), narrow),
+            pltpu.VMEM((windows, 2, cells, cells), narrow),
+            pltpu.VMEM((windows, 2, cells, cells), narrow),
+            pltpu.VMEM((scalars[0].shape[0], cells, cells), wide),
+            pltpu.SemaphoreType.DMA((STAGES,)),
+            pltpu.SemaphoreType.DMA,
+            pltpu.SemaphoreType.DMA,
+            pltpu.SemaphoreType.DMA((3,)),
+            pltpu.SemaphoreType.DMA((3,)),
+            pltpu.SemaphoreType.DMA((2, 8 * SIDE)),
+            pltpu.SemaphoreType.DMA((2, 8 * SIDE)),
+        ],
+        compiler_params=pltpu.CompilerParams(
+            collective_id=1, has_side_effects=True, vmem_limit_bytes=60 << 20
+        ),
+        name="gather",
+    )(
+        *scalars, object_field, amplitudes.reshape(own), probe_field, *tables
+    )
+
+
 def local(object_field, probe_field, amplitudes, scan_blocks, owner_rows):
     tile_rows, tile_cols = object_field.shape[1:]
     window_cells = probe_field.shape[1]
@@ -345,14 +608,6 @@
     pair_slots = amplitudes.shape[0] // lax.axis_size("tx")
     spots = tile_cols // block_cells
     windows = tile_rows // block_cells * spots
-    ext_rows, ext_cols = tile_rows + block_cells, tile_cols + block_cells
-
-    lower_rows = from_behind(object_field[:, :block_cells, :], "tx", -1)
-    taller = jnp.concatenate([object_field, lower_rows], axis=1)
-    right_cols = from_behind(taller[:, :, :block_cells], "ty", -1)
-    extended = jnp.concatenate([taller, right_cols], axis=2)
-    outgoing, extended = lax.optimization_barrier((amplitudes.astype(jnp.bfloat16), extended))
-    arrived = lax.all_to_all(outgoing, "tx", split_axis=0, concat_axis=0, tiled=True)
 
     order = jnp.arange(positions_here, dtype=jnp.int32)
     earlier = order[None, :] < order[:, None]
@@ -369,50 +624,18 @@
     slots = jnp.sum(
         jnp.where(place[None, :] == order[:, None], slot_index[None, :], 0), axis=1
     ).astype(jnp.int32)
-    bounds = jnp.arange(windows + 1, dtype=jnp.int32)
-    starts = jnp.sum(window_index[None, :] < bounds[:, None], axis=1).astype(jnp.int32)
-
-    ahead, conjugate = complex_tables(window_cells)
-    plane = (2, window_cells, window_cells)
-    per_window = pl.BlockSpec((1, *plane), lambda number, *_: (number, 0, 0, 0))
-    kept = jax.ShapeDtypeStruct((windows, *plane), jnp.bfloat16)
-    flops = windows * 16 * window_cells**3
-    far, phase = pl.pallas_call(
-        functools.partial(forward_kernel, spots),
-        grid=(windows,),
-        out_shape=(kept, kept),
-        in_specs=[whole(extended.shape), whole(plane), whole(ahead.shape), whole(ahead.shape)],
-        out_specs=(per_window, per_window),
-        cost_estimate=pl.CostEstimate(
-            flops=flops, bytes_accessed=12 << 20, transcendentals=windows * window_cells**2
-        ),
-        name="forward",
-    )(extended, probe_field, ahead, conjugate)
-
-    gradient_sum = pl.pallas_call(
-        functools.partial(backward_kernel, spots),
-        out_shape=jax.ShapeDtypeStruct((2, ext_rows, ext_cols), jnp.float32),
-        grid_spec=pltpu.PrefetchScalarGridSpec(
-            num_scalar_prefetch=2,
-            grid=(windows,),
-            in_specs=[
-                per_window,
-                per_window,
-                pl.BlockSpec(
-                    arrived.shape, lambda *_: (0, 0, 0), pipeline_mode=pl.Buffered(1)
-                ),
-                whole(plane),
-                whole(ahead.shape),
-                whole(ahead.shape),
-            ],
-            out_specs=whole((2, ext_rows, ext_cols)),
-            scratch_shapes=[pltpu.VMEM((window_cells, window_cells), jnp.float32)],
-        ),
-        cost_estimate=pl.CostEstimate(flops=flops, bytes_accessed=24 << 20, transcendentals=0),
-        name="backward",
-    )(slots, starts, far, phase, arrived, probe_field, ahead, conjugate)
-
-    counts = (starts[1:] - starts[:-1]).astype(jnp.float32)
+    bounds = jnp.arange(windows, dtype=jnp.int32)
+    counts = jnp.sum(window_index[None, :] == bounds[:, None], axis=1).astype(jnp.float32)
+    ends = jnp.sum(window_index[None, :] <= bounds[:, None], axis=1).astype(jnp.int32)
+    follows = (window_index[None, :] == window_index[:, None]) & earlier
+    same = jnp.sum(
+        jnp.where(place[None, :] == order[:, None], jnp.any(follows, axis=1)[None, :], False),
+        axis=1,
+    ).astype(jnp.int32)
+    scalars = (slots, same, jnp.maximum(ends - 1, 0), counts)
+    gradient_sum = gather(
+        object_field, probe_field, amplitudes, complex_tables(window_cells), scalars
+    )
     counts = jnp.broadcast_to(counts[:, None], (windows, LANES))
     return finish(object_field, gradient_sum, probe_field, counts)
 

time: 234 us -> 172 us (0.74)
  waiting for transfers between devices: 82.3 us -> 0 us
  Pallas kernels: 117 us -> 163 us
  starting transfers between devices: 16.5 us -> 0 us
  other arithmetic: 11.2 us -> 3.87 us
  local copies, waits for them, and re-layouts: 4.37 us -> 1.4 us
    all_to_all x1 -> x0, waiting for transfers between devices: 71.8 us -> none  [local(): lax.all_to_all(outgoing, 'tx', split_axis=0, concat_axis=0, tiled=True)]
    pallas_call x2 -> x1, Pallas kernels: 34.4 us -> 98.2 us  [gather(): pl.pallas_call(functools.partial(gather_kernel, sizes), out_shape=jax.Sha...]
    pallas_call x1, Pallas kernels: 82.6 us -> 65.1 us  [finish(): pl.pallas_call(functools.partial(finish_kernel, sizes), out_shape=jax.Sha...]
    ppermute x2 -> x0, waiting for transfers between devices: 10.5 us -> none  [from_behind(): lax.ppermute(value, axis, [(source, source + steps) for source in range(i...]
    ppermute x2 -> x0, starting transfers between devices: 8.35 us -> none  [from_behind(): lax.ppermute(value, axis, [(source, source + steps) for source in range(i...]
    convert_element_type x2 -> x1, other arithmetic: 8.19 us -> 0.01 us  [local(): jnp.sum(window_index[None, :] == bounds[:, None], axis=1)]
    all_to_all x1 -> x0, starting transfers between devices: 8.13 us -> none  [local(): lax.all_to_all(outgoing, 'tx', split_axis=0, concat_axis=0, tiled=True)]
  transfers between devices with their start and end apart: 3 -> 0, of which waited for: 3 -> 0; matrix products, arithmetic and copies ran while one was open for 5% -> 0% of each run, Pallas kernels for 7% -> 0%
where the time goes in v3:
time: 172 us; the launch traced here: 169 us
  Pallas kernels  163 us (95%)
  other arithmetic  3.87 us (2%)
    pallas_call x1, Pallas kernels, gather(): pl.pallas_call(functools.partial(gather_kernel, sizes), out_shape=jax.Sha...  98.2 us
    pallas_call x1, Pallas kernels, finish(): pl.pallas_call(functools.partial(finish_kernel, sizes), out_shape=jax.Sha...  65.1 us

profile of v3, /device:TPU:7, one launch (start us, length us, event | category | flops | bytes accessed | tf_op | source)
XLA Modules:
  0.0 168.7 jit_solution(11142293536262868358)
XLA Ops:
  0.0 0.8 subtract_bitcast_fusion
  0.8 0.2 fusion.3
  0.9 0.9 convert_reduce_fusion.3
  1.9 0.7 multiply_add_fusion
  2.5 0.2 convert_reduce_fusion
  2.7 0.0 copy-start.2
  2.7 0.6 convert_reduce_fusion.2
  3.4 0.5 add_maximum_fusion.ends
  3.9 0.1 broadcast_in_dim.26.counts
  4.0 0.0 copy-done.2
  4.0 0.0 copy-start
  4.0 0.0 copy-start.1
  4.0 98.2 %gather.1.grads = f32[2,640,640]{2,1,0:T(8,128)} custom-call(s32[16]{0:T(128)} %get-tuple-element.9.slots, s32[16]{0:T(128)} %get-tuple-element.8.same, s32[16]{0:T(128)} %add_maximum_fusion.ends, f32[16]{0:T(128)} %copy-done.2, f32[2,512,512]{2,1,0:T(8,128)} %field.3, f32[16,3,256,256]{3,2,1,0:T(8,128)} %bitcast.3, f32[2,256,256]{2,1,0:T(8,128)} %probe.3, ...), custom_call_target="tpu_custom_call" | custom-call | tf_op jit(solution)/shard_map/gather/pallas_call | solution.py:568
  102.2 0.0 copy-done
  102.2 0.0 copy-done.1
  102.2 65.1 %finish.1 = f32[2,512,512]{2,1,0:T(8,128)S(1)} custom-call(f32[2,512,512]{2,1,0:T(8,128)S(1)} %copy-done, f32[2,640,640]{2,1,0:T(8,128)} %gather.1.grads, f32[2,256,256]{2,1,0:T(8,128)S(1)} %copy-done.1, f32[16,128]{1,0:T(8,128)S(1)} %broadcast_in_dim.26.counts), custom_call_target="tpu_custom_call" | custom-call | tf_op jit(solution)/shard_map/finish/pallas_call | solution.py:239
  167.3 1.3 copy.9
  (1 shorter events, 0.0 us)
Async XLA Ops:
  2.7 1.3 copy-start.2
  4.0 98.2 %copy-start = (f32[2,512,512]{2,1,0:T(8,128)S(1)}, f32[2,512,512]{2,1,0:T(8,128)}, u32[]{:S(2)}) copy-start(f32[2,512,512]{2,1,0:T(8,128)} %field.3) | copy-start | bytes 6291460
  4.0 98.2 %copy-start.1 = (f32[2,256,256]{2,1,0:T(8,128)S(1)}, f32[2,256,256]{2,1,0:T(8,128)}, u32[]{:S(2)}) copy-start(f32[2,256,256]{2,1,0:T(8,128)} %probe.3) | copy-start | bytes 1572868

commit v4 on v3

--- a/solution.py
+++ b/solution.py
@@ -33,234 +33,15 @@
 
 LANES = 128
 RIM = 8
+UNROLL = 6
 MESH = pl.DeviceIdType.MESH
 ONWARD = ((1, 0), (0, 1), (1, 1))
 AROUND = ((-1, 0), (1, 0), (0, -1), (0, 1), (-1, -1), (-1, 1), (1, -1), (1, 1))
 
 
-def flux(difference):
-    weight = 1.0 / (
-        1.0 + (difference[0] * difference[0] + difference[1] * difference[1]) * (1.0 / KAPPA_SQ)
-    )
-    return weight[None] * difference
-
-
-def finish_kernel(
-    sizes, field, grads, probe, counts, out,
-    sent_down, sent_right, sent_corner, got_down, got_right, got_corner, got_counts,
-    inverse, column_rims, got_rows, got_columns, got_corners, first, second,
-    send_sem, recv_sem, rim_send_sem, rim_recv_sem,
-):
-    n_tx, n_ty = sizes
-    rows, cols = field.shape[1:]
-    block = probe.shape[1] // 2
-    spots = cols // block
-    row, col = lax.axis_index("tx"), lax.axis_index("ty")
-
-    def device(step):
-        return (lax.rem(row + step[0] + n_tx, n_tx), lax.rem(col + step[1] + n_ty, n_ty))
-
-    barrier = pltpu.get_barrier_semaphore()
-    for step in AROUND:
-        pl.semaphore_signal(barrier, inc=1, device_id=device(step), device_id_type=MESH)
-
-    sent_down[...] = grads[:, rows:, :cols].astype(jnp.bfloat16)
-    sent_right[...] = grads[:, :rows, cols:].astype(jnp.bfloat16)
-    sent_corner[...] = grads[:, rows:, cols:].astype(jnp.bfloat16)
-    pl.semaphore_wait(barrier, len(AROUND))
-
-    def send(source, target, sems, number, step):
-        return pltpu.make_async_remote_copy(
-            src_ref=source,
-            dst_ref=target,
-            send_sem=sems[0].at[number],
-            recv_sem=sems[1].at[number],
-            device_id=device(step),
-            device_id_type=MESH,
-        )
-
-    sums = (send_sem, recv_sem)
-    sum_copies = [
-        send(source, target, sums, number, ONWARD[number])
-        for number, (source, target) in enumerate(
-            ((sent_down, got_down), (sent_right, got_right), (sent_corner, got_corner))
-        )
-    ]
-    count_copies = [
-        send(counts, got_counts.at[number], sums, 3 + number, step)
-        for number, step in enumerate(ONWARD)
-    ]
-    for copy in count_copies + sum_copies:
-        copy.start()
-
-    has_above, has_left = row > 0, col > 0
-    has_below, has_right = row < n_tx - 1, col < n_ty - 1
-    above, left = has_above.astype(jnp.float32), has_left.astype(jnp.float32)
-    for copy in count_copies:
-        copy.wait()
-
-    def count_of(block_row, block_col):
-        number = block_row % spots * spots + block_col % spots
-        if block_row < 0 and block_col < 0:
-            return got_counts[2, number : number + 1, :] * (above * left)
-        if block_row < 0:
-            return got_counts[0, number : number + 1, :] * above
-        if block_col < 0:
-            return got_counts[1, number : number + 1, :] * left
-        return counts[number : number + 1, :]
-
-    for block_row in range(rows // block):
-        for block_col in range(spots):
-            light = jnp.ones((block, block), jnp.float32)
-            for down in range(2):
-                for right in range(2):
-                    part = (pl.ds(down * block, block), pl.ds(right * block, block))
-                    power = probe[(0, *part)] ** 2 + probe[(1, *part)] ** 2
-                    light += count_of(block_row - down, block_col - right) * power
-            inverse[pl.ds(block_row * block, block), pl.ds(block_col * block, block)] = 1.0 / light
-
-    for copy in sum_copies:
-        copy.wait()
-    for part in range(2):
-        grads[part, :block, :cols] += got_down[part].astype(jnp.float32) * above
-        grads[part, :rows, :block] += got_right[part].astype(jnp.float32) * left
-        grads[part, :block, :block] += got_corner[part].astype(jnp.float32) * (above * left)
-        updated = field[part] - grads[part, :rows, :cols] * inverse[...]
-        first[part, pl.ds(2 * RIM, rows), pl.ds(0, cols)] = updated
-        column_rims[0, part] = updated[:, :LANES].T[:RIM]
-        column_rims[1, part] = updated[:, cols - LANES :].T[LANES - RIM :]
-
-    rims = (rim_send_sem, rim_recv_sem)
-    top, bottom = pl.ds(2 * RIM, RIM), pl.ds(2 * RIM + rows - RIM, RIM)
-    west, east = pl.ds(0, LANES), pl.ds(cols - LANES, LANES)
-    sources = (
-        (first.at[:, top, pl.ds(0, cols)], got_rows.at[1]),
-        (first.at[:, bottom, pl.ds(0, cols)], got_rows.at[0]),
-        (column_rims.at[0], got_columns.at[1]),
-        (column_rims.at[1], got_columns.at[0]),
-        (first.at[:, top, west], got_corners.at[3]),
-        (first.at[:, top, east], got_corners.at[2]),
-        (first.at[:, bottom, west], got_corners.at[1]),
-        (first.at[:, bottom, east], got_corners.at[0]),
-    )
-    rim_copies = [
-        send(source, target, rims, number, AROUND[number])
-        for number, (source, target) in enumerate(sources)
-    ]
-    for copy in rim_copies:
-        copy.start()
-    for copy in rim_copies:
-        copy.wait()
-
-    lanes = lax.broadcasted_iota(jnp.int32, (RIM, LANES), 1)
-    on_right = lanes < jnp.where(has_right, RIM, 0)
-    on_left = lanes >= jnp.where(has_left, LANES - RIM, LANES)
-    zero = jnp.zeros((), jnp.float32)
-    extra = pl.ds(cols, LANES)
-    for part in range(2):
-        for number, place, exists in ((0, RIM, has_above), (1, 2 * RIM + rows, has_below)):
-            corner = jnp.where(
-                on_left, got_corners[2 * number, part],
-                jnp.where(on_right, got_corners[2 * number + 1, part], zero),
-            )
-            first[part, pl.ds(place, RIM), pl.ds(0, cols)] = jnp.where(
-                exists, got_rows[number, part], zero
-            )
-            first[part, pl.ds(place, RIM), extra] = jnp.where(exists, corner, zero)
-        sides = jnp.concatenate(
-            [
-                jnp.where(has_right, got_columns[1, part], zero),
-                jnp.zeros((LANES - 2 * RIM, rows), jnp.float32),
-                jnp.where(has_left, got_columns[0, part], zero),
-            ],
-            axis=0,
-        )
-        first[part, pl.ds(2 * RIM, rows), extra] = sides.T
-
-    wide = cols + LANES
-    every = lax.broadcasted_iota(jnp.int32, (RIM, wide), 1)
-    lane_kept = (every < jnp.where(has_right, cols + RIM, cols)) | (
-        every >= jnp.where(has_left, wide - RIM, wide)
-    )
-    sublane = lax.broadcasted_iota(jnp.int32, (2, RIM, wide), 1)
-    chunks = rows // RIM + 2
-
-    def smooth(source, store, start, stop):
-        def chunk(number, earlier):
-            place = pl.multiple_of((number + 1) * RIM, RIM)
-            center = source[:, pl.ds(place, RIM), :]
-            below = source[:, pl.ds(pl.multiple_of(place + RIM, RIM), RIM), :]
-            lower = jnp.where(
-                sublane == RIM - 1,
-                pltpu.roll(below, RIM - 1, axis=1),
-                pltpu.roll(center, RIM - 1, axis=1),
-            )
-            down = flux(lower - center)
-            up = jnp.where(
-                sublane == 0, pltpu.roll(earlier, 1, axis=1), pltpu.roll(down, 1, axis=1)
-            )
-            right = flux(pltpu.roll(center, wide - 1, axis=2) - center)
-            left_flux = pltpu.roll(right, 1, axis=2)
-            store(number, place, center + TIME_STEP * ((down - up) + (right - left_flux)))
-            return down
-
-        lax.fori_loop(start, stop, chunk, jnp.zeros((2, RIM, wide), jnp.float32))
-
-    def keep(target):
-        def store(number, place, value):
-            exists = jnp.where(
-                number == 0, has_above, jnp.where(number == chunks - 1, has_below, True)
-            )
-            kept = lane_kept & exists
-            target[:, pl.ds(place, RIM), :] = jnp.where(kept[None], value, zero)
-
-        return store
-
-    def give(number, place, value):
-        target = pl.multiple_of(place - 2 * RIM, RIM)
-        @pl.when(number > 0)
-        def _():
-            out[:, pl.ds(target, RIM), :] = value[:, :, :cols]
-
-    now, later = first, second
-    for _ in range(STEPS - 1):
-        smooth(now, keep(later), 0, chunks)
-        now, later = later, now
-    smooth(now, give, 0, chunks - 1)
-
-
-def finish(object_field, gradient_sum, probe_field, counts):
-    rows, cols = object_field.shape[1:]
-    block = probe_field.shape[1] // 2
-    sizes = (lax.axis_size("tx"), lax.axis_size("ty"))
-    tall, wide = rows + 4 * RIM, cols + LANES
-    strips = [(2, block, cols), (2, rows, block), (2, block, block)]
-    vmem = pl.BlockSpec(memory_space=pltpu.VMEM)
-    return pl.pallas_call(
-        functools.partial(finish_kernel, sizes),
-        out_shape=jax.ShapeDtypeStruct(object_field.shape, jnp.float32),
-        in_specs=[vmem] * 4,
-        out_specs=vmem,
-        scratch_shapes=[
-            *(pltpu.VMEM(strip, jnp.bfloat16) for strip in strips * 2),
-            pltpu.VMEM((3, *counts.shape), jnp.float32),
-            pltpu.VMEM((rows, cols), jnp.float32),
-            pltpu.VMEM((2, 2, RIM, rows), jnp.float32),
-            pltpu.VMEM((2, 2, RIM, cols), jnp.float32),
-            pltpu.VMEM((2, 2, RIM, rows), jnp.float32),
-            pltpu.VMEM((4, 2, RIM, LANES), jnp.float32),
-            pltpu.VMEM((2, tall, wide), jnp.float32),
-            pltpu.VMEM((2, tall, wide), jnp.float32),
-            pltpu.SemaphoreType.DMA((6,)),
-            pltpu.SemaphoreType.DMA((6,)),
-            pltpu.SemaphoreType.DMA((8,)),
-            pltpu.SemaphoreType.DMA((8,)),
-        ],
-        compiler_params=pltpu.CompilerParams(
-            collective_id=0, has_side_effects=True, vmem_limit_bytes=48 << 20
-        ),
-        name="finish",
-    )(object_field, gradient_sum, probe_field, counts)
+def flux(real, imag):
+    weight = 1.0 / (1.0 + (real * real + imag * imag) * (1.0 / KAPPA_SQ))
+    return weight * real, weight * imag
 
 
 SIDE = 4
@@ -271,13 +52,16 @@
         key=lambda step: (step == (0, 0), 2 not in step, 0 in step),
     )
 )
-NEARBY = ((1, 0), (-1, 0), (0, 1), (0, -1), (1, 1), (-1, -1))
-
-
-def gather_kernel(
-    sizes, slots, same, ends, counts, field, amplitudes, probe, ahead, conjugate, grads,
+
+
+def step_kernel(
+    sizes, slots, same, ends, counts, field, amplitudes, probe, ahead, conjugate, wide_counts, out,
     extended, sent_rows, got_rows, staged, sent, arrived, held, passed, passed_again,
-    far, phase, sums, stage_sem, field_sem, own_sem, halo_send, halo_recv, send_sem, recv_sem,
+    far, phase, sums, grads, inverse, got_counts,
+    sent_down, sent_right, sent_corner, got_down, got_right, got_corner,
+    column_rims, got_tops, got_columns, got_corners, first_field, second_field,
+    stage_sem, field_sem, own_sem, halo_send, halo_recv, send_sem, recv_sem,
+    sum_send, sum_recv, rim_send, rim_recv,
 ):
     n_tx, n_ty = sizes
     cells = probe.shape[1]
@@ -311,7 +95,7 @@
         load(number).start()
 
     barrier = pltpu.get_barrier_semaphore()
-    partners = [around(step) for step in NEARBY] + [
+    partners = [around(step) for step in AROUND] + [
         (owner_at(half, place[half] + step, place[1 - half]), col)
         for half in range(2)
         for step in (1, -1)
@@ -388,6 +172,14 @@
         ),
     ]
 
+    halos += [
+        remote(
+            wide_counts, got_counts.at[number],
+            (halo_send.at[3 + number], halo_recv.at[3 + number]), around(step),
+        )
+        for number, step in enumerate(ONWARD)
+    ]
+
     for number, (dx, dy) in enumerate(TAKEN):
         slot = number % STAGES
         home = owner_at(0, place[0] + dx, place[1] + dy)
@@ -469,6 +261,30 @@
         def _():
             extended[(slice(None), *corner)] = jnp.zeros((2, block, block), jnp.float32)
 
+    above, left = (row > 0).astype(jnp.float32), (col > 0).astype(jnp.float32)
+
+    def count_of(block_row, block_col):
+        number = block_row % spots * spots + block_col % spots
+        if block_row < 0 and block_col < 0:
+            return got_counts[2, number : number + 1, :] * (above * left)
+        if block_row < 0:
+            return got_counts[0, number : number + 1, :] * above
+        if block_col < 0:
+            return got_counts[1, number : number + 1, :] * left
+        return wide_counts[number : number + 1, :]
+
+    def light_up():
+        for block_row in range(rows // block):
+            for block_col in range(spots):
+                light = jnp.ones((block, block), jnp.float32)
+                for down in range(2):
+                    for right in range(2):
+                        part = (pl.ds(down * block, block), pl.ds(right * block, block))
+                        power = probe[(0, *part)] ** 2 + probe[(1, *part)] ** 2
+                        light += count_of(block_row - down, block_col - right) * power
+                spot = (pl.ds(block_row * block, block), pl.ds(block_col * block, block))
+                inverse[spot] = 1.0 / light
+
     inner = spots - 1
     steps = {
         3: [relay_first],
@@ -499,8 +315,10 @@
     for second in (2, 1, 3):
         turn(2, second)
     grads[...] = jnp.zeros_like(grads)
-    for first in (0, 1, 3, 2):
+    for first in (0, 1, 3):
         relay_second(first)
+    light_up()
+    relay_second(2)
 
     own.wait()
     for half in range(2):
@@ -519,7 +337,32 @@
 
     lax.fori_loop(0, sums.shape[0], add_up, 0)
 
-    def backward(number, carry):
+    sum_copies = [
+        remote(source, target, (sum_send.at[number], sum_recv.at[number]), around(ONWARD[number]))
+        for number, (source, target) in enumerate(
+            ((sent_down, got_down), (sent_right, got_right), (sent_corner, got_corner))
+        )
+    ]
+
+    def backward(index, carry):
+        interior = index - 2 * spots + 1
+        edge = interior < 0
+        at_row = jnp.where(
+            edge, jnp.where(index < spots, inner, index - spots), interior // inner
+        )
+        at_col = jnp.where(
+            edge, jnp.where(index < spots, index, inner), lax.rem(interior, inner)
+        )
+        number = at_row * spots + at_col
+
+        @pl.when(index == 2 * spots - 1)
+        def _():
+            sent_down[...] = grads[:, rows:, :cols].astype(jnp.bfloat16)
+            sent_right[...] = grads[:, :rows, cols:].astype(jnp.bfloat16)
+            sent_corner[...] = grads[:, rows:, cols:].astype(jnp.bfloat16)
+            for copy in sum_copies:
+                copy.start()
+
         count = counts[number]
         total = sums[ends[number]] * jnp.minimum(count, 1.0)
         residual = [
@@ -533,14 +376,160 @@
         near = matmul(jnp.concatenate([back[:cells], back[cells:]], axis=1), ahead[...])
         near_re, near_im = near[:, :cells], near[:, cells:]
         probe_re, probe_im = probe[0], probe[1]
-        start_row = pl.multiple_of(number // spots * block, block)
-        start_col = pl.multiple_of(lax.rem(number, spots) * block, block)
-        view = (pl.ds(start_row, cells), pl.ds(start_col, cells))
+        view = (
+            pl.ds(pl.multiple_of(at_row * block, block), cells),
+            pl.ds(pl.multiple_of(at_col * block, block), cells),
+        )
         grads[(0, *view)] += probe_re * near_re + probe_im * near_im
         grads[(1, *view)] += probe_re * near_im - probe_im * near_re
         return carry
 
     lax.fori_loop(0, windows, backward, 0)
+    strips = cols // LANES
+    for copy in sum_copies:
+        copy.wait()
+    for part in range(2):
+        grads[part, :block, :cols] += got_down[part].astype(jnp.float32) * above
+        grads[part, :rows, :block] += got_right[part].astype(jnp.float32) * left
+        grads[part, :block, :block] += got_corner[part].astype(jnp.float32) * (above * left)
+        for strip in range(strips):
+            lanes = pl.ds(strip * LANES, LANES)
+            updated = (
+                extended[part, pl.ds(0, rows), lanes]
+                - grads[part, pl.ds(0, rows), lanes] * inverse[:, lanes]
+            )
+            first_field[part, strip, pl.ds(2 * RIM, rows), :] = updated
+            if strip == 0:
+                column_rims[0, part] = updated.T[:RIM]
+            if strip == strips - 1:
+                column_rims[1, part] = updated.T[LANES - RIM :]
+
+    top, bottom = pl.ds(2 * RIM, RIM), pl.ds(2 * RIM + rows - RIM, RIM)
+    main = pl.ds(0, strips)
+    rim_copies = [
+        remote(source, target, (rim_send.at[number], rim_recv.at[number]), around(AROUND[number]))
+        for number, (source, target) in enumerate(
+            (
+                (first_field.at[:, main, top], got_tops.at[1]),
+                (first_field.at[:, main, bottom], got_tops.at[0]),
+                (column_rims.at[0], got_columns.at[1]),
+                (column_rims.at[1], got_columns.at[0]),
+                (first_field.at[:, 0, top], got_corners.at[3]),
+                (first_field.at[:, strips - 1, top], got_corners.at[2]),
+                (first_field.at[:, 0, bottom], got_corners.at[1]),
+                (first_field.at[:, strips - 1, bottom], got_corners.at[0]),
+            )
+        )
+    ]
+    for copy in rim_copies:
+        copy.start()
+    for copy in rim_copies:
+        copy.wait()
+
+    has_above, has_left = row > 0, col > 0
+    has_below, has_right = row < n_tx - 1, col < n_ty - 1
+    lane = lax.broadcasted_iota(jnp.int32, (RIM, LANES), 1)
+    sublane = lax.broadcasted_iota(jnp.int32, (RIM, LANES), 0)
+    on_right = lane < jnp.where(has_right, RIM, 0)
+    on_left = lane >= jnp.where(has_left, LANES - RIM, LANES)
+    beside = on_right | on_left
+    ends_of_tile = ((0, RIM, has_above), (1, 2 * RIM + rows, has_below))
+    for part in range(2):
+        for number, start, exists in ends_of_tile:
+            corner_cells = jnp.where(
+                on_left, got_corners[2 * number, part],
+                jnp.where(on_right, got_corners[2 * number + 1, part], 0.0),
+            )
+            spot = pl.ds(start, RIM)
+            for strip in range(strips):
+                first_field[part, strip, spot, :] = jnp.where(
+                    exists, got_tops[number, part, strip], 0.0
+                )
+            first_field[part, strips, spot, :] = jnp.where(exists, corner_cells, 0.0)
+        sides = jnp.concatenate(
+            [
+                jnp.where(has_right, got_columns[1, part], 0.0),
+                jnp.zeros((LANES - 2 * RIM, rows), jnp.float32),
+                jnp.where(has_left, got_columns[0, part], 0.0),
+            ],
+            axis=0,
+        )
+        first_field[part, strips, pl.ds(2 * RIM, rows), :] = sides.T
+
+    everywhere = [(part, strip) for strip in range(strips + 1) for part in range(2)]
+    blank = jnp.zeros((RIM, LANES), jnp.float32)
+
+    def smooth(source, store, start, stop):
+        def shifted(values, amount, edge):
+            turned = {key: pltpu.roll(value, amount, axis=1) for key, value in values.items()}
+            step = 1 if edge else -1
+            return {
+                (part, strip): jnp.where(
+                    lane == edge, turned[part, (strip + step) % (strips + 1)], turned[part, strip]
+                )
+                for part, strip in everywhere
+            }
+
+        def fluxes(ahead_of, center):
+            found = {}
+            for strip in range(strips + 1):
+                found[0, strip], found[1, strip] = flux(
+                    *(ahead_of[part, strip] - center[part, strip] for part in range(2))
+                )
+            return found
+
+        def chunk(number, earlier):
+            start_row = pl.multiple_of((number + 1) * RIM, RIM)
+            center, lower = (
+                {
+                    (part, strip): source[part, strip, pl.ds(start_row + offset, RIM), :]
+                    for part, strip in everywhere
+                }
+                for offset in (0, 1)
+            )
+            down = fluxes(lower, center)
+            right = fluxes(shifted(center, LANES - 1, LANES - 1), center)
+            before = shifted(right, 1, 0)
+            for at, key in enumerate(everywhere):
+                up = jnp.where(
+                    sublane == 0,
+                    pltpu.roll(earlier[at], 1, axis=0),
+                    pltpu.roll(down[key], 1, axis=0),
+                )
+                value = center[key] + TIME_STEP * ((down[key] - up) + (right[key] - before[key]))
+                store(start_row, *key, value)
+            return [down[key] for key in everywhere]
+
+        lax.fori_loop(start, stop, chunk, [blank] * len(everywhere), unroll=UNROLL)
+
+    def keep(target):
+        def store(start_row, part, strip, value):
+            if strip == strips:
+                value = jnp.where(beside, value, 0.0)
+            target[part, strip, pl.ds(start_row, RIM), :] = value
+
+        return store
+
+    def give(start_row, part, strip, value):
+        if strip < strips:
+            target = pl.multiple_of(jnp.maximum(start_row - 2 * RIM, 0), RIM)
+            out[part, pl.ds(target, RIM), pl.ds(strip * LANES, LANES)] = value
+
+    chunks = rows // RIM + 2
+    now, later = first_field, second_field
+    for _ in range(STEPS - 1):
+        smooth(now, keep(later), 0, chunks)
+        for _, start, exists in ends_of_tile:
+
+            @pl.when(jnp.logical_not(exists))
+            def _(start=start, later=later):
+                later[:, :, pl.ds(start, RIM), :] = jnp.zeros(
+                    (2, strips + 1, RIM, LANES), jnp.float32
+                )
+
+        now, later = later, now
+    smooth(now, give, 0, chunks - 1)
+
     for half in range(2):
         for kind in range(4):
             for second in range(SIDE):
@@ -550,7 +539,7 @@
                 piece(half, kind, first, None).wait_send()
 
 
-def gather(object_field, probe_field, amplitudes, tables, scalars):
+def whole_step(object_field, probe_field, amplitudes, tables, scalars, wide_counts):
     rows, cols = object_field.shape[1:]
     cells = probe_field.shape[1]
     block = cells // 2
@@ -565,10 +554,12 @@
     narrow, wide = jnp.bfloat16, jnp.float32
     own = (groups, slots, cells, cells)
     part = (slots, block, cells)
+    strips = [(2, block, cols), (2, rows, block), (2, block, block)]
+    smoothed = (2, cols // LANES + 1, rows + 4 * RIM, LANES)
     return pl.pallas_call(
-        functools.partial(gather_kernel, sizes),
-        out_shape=jax.ShapeDtypeStruct((2, rows + block, cols + block), wide),
-        in_specs=[smem] * 4 + [anywhere] * 2 + [vmem] * 3,
+        functools.partial(step_kernel, sizes),
+        out_shape=jax.ShapeDtypeStruct(object_field.shape, wide),
+        in_specs=[smem] * 4 + [anywhere] * 2 + [vmem] * 4,
         out_specs=vmem,
         scratch_shapes=[
             pltpu.VMEM((2, rows + block, cols + block), wide),
@@ -583,20 +574,34 @@
             pltpu.VMEM((windows, 2, cells, cells), narrow),
             pltpu.VMEM((windows, 2, cells, cells), narrow),
             pltpu.VMEM((scalars[0].shape[0], cells, cells), wide),
+            pltpu.VMEM((2, rows + block, cols + block), wide),
+            pltpu.VMEM((rows, cols), wide),
+            pltpu.VMEM((3, *wide_counts.shape), wide),
+            *(pltpu.VMEM(strip, narrow) for strip in strips * 2),
+            pltpu.VMEM((2, 2, RIM, rows), wide),
+            pltpu.VMEM((2, 2, cols // LANES, RIM, LANES), wide),
+            pltpu.VMEM((2, 2, RIM, rows), wide),
+            pltpu.VMEM((4, 2, RIM, LANES), wide),
+            pltpu.VMEM(smoothed, wide),
+            pltpu.VMEM(smoothed, wide),
             pltpu.SemaphoreType.DMA((STAGES,)),
             pltpu.SemaphoreType.DMA,
             pltpu.SemaphoreType.DMA,
+            pltpu.SemaphoreType.DMA((6,)),
+            pltpu.SemaphoreType.DMA((6,)),
+            pltpu.SemaphoreType.DMA((2, 8 * SIDE)),
+            pltpu.SemaphoreType.DMA((2, 8 * SIDE)),
             pltpu.SemaphoreType.DMA((3,)),
             pltpu.SemaphoreType.DMA((3,)),
-            pltpu.SemaphoreType.DMA((2, 8 * SIDE)),
-            pltpu.SemaphoreType.DMA((2, 8 * SIDE)),
+            pltpu.SemaphoreType.DMA((8,)),
+            pltpu.SemaphoreType.DMA((8,)),
         ],
         compiler_params=pltpu.CompilerParams(
             collective_id=1, has_side_effects=True, vmem_limit_bytes=60 << 20
         ),
-        name="gather",
+        name="step",
     )(
-        *scalars, object_field, amplitudes.reshape(own), probe_field, *tables
+        *scalars, object_field, amplitudes.reshape(own), probe_field, *tables, wide_counts
     )
 
 
@@ -633,11 +638,9 @@
         axis=1,
     ).astype(jnp.int32)
     scalars = (slots, same, jnp.maximum(ends - 1, 0), counts)
-    gradient_sum = gather(
-        object_field, probe_field, amplitudes, complex_tables(window_cells), scalars
-    )
-    counts = jnp.broadcast_to(counts[:, None], (windows, LANES))
-    return finish(object_field, gradient_sum, probe_field, counts)
+    wide_counts = jnp.broadcast_to(counts[:, None], (windows, LANES))
+    tables = complex_tables(window_cells)
+    return whole_step(object_field, probe_field, amplitudes, tables, scalars, wide_counts)
 
 
 def solution(mesh):

time: 172 us -> 130 us (0.76)
  Pallas kernels: 163 us -> 120 us
  local copies, waits for them, and re-layouts: 1.4 us -> 3.75 us
    pallas_call x2 -> x1, Pallas kernels: 163 us -> 120 us  [whole_step(): pl.pallas_call(functools.partial(step_kernel, sizes), out_shape=jax.Shape...]
    unnamed x7 -> x3, local copies, waits for them, and re-layouts: 1.33 us -> 3.08 us
where the time goes in v4:
time: 130 us; the launch traced here: 128 us
  Pallas kernels  120 us (92%)
  other arithmetic  3.88 us (3%)
  local copies, waits for them, and re-layouts  3.75 us (3%)
    pallas_call x1, Pallas kernels, whole_step(): pl.pallas_call(functools.partial(step_kernel, sizes), out_shape=jax.Shape...  120 us
    unnamed x3, local copies, waits for them, and re-layouts  3.08 us

profile of v4, /device:TPU:7, one launch (start us, length us, event | category | flops | bytes accessed | tf_op | source)
XLA Modules:
  0.0 128.0 jit_solution(8105963533220025274)
XLA Ops:
  0.0 0.8 subtract_bitcast_fusion
  0.8 0.2 fusion.3
  0.9 0.9 convert_reduce_fusion.3
  1.9 0.7 multiply_add_fusion
  2.5 0.2 convert_reduce_fusion
  2.7 0.0 copy-start
  2.7 0.7 convert_reduce_fusion.2
  3.4 0.5 add_maximum_fusion.ends
  3.9 0.7 broadcast_in_dim.26.wide_counts
  4.6 0.0 copy-done
  4.6 120.3 %step.1 = f32[2,512,512]{2,1,0:T(8,128)} custom-call(s32[16]{0:T(128)} %get-tuple-element.9.slots, s32[16]{0:T(128)} %get-tuple-element.8.same, s32[16]{0:T(128)} %add_maximum_fusion.ends, f32[16]{0:T(128)} %copy-done, f32[2,512,512]{2,1,0:T(8,128)} %field.1, f32[16,3,256,256]{3,2,1,0:T(8,128)} %bitcast.3, f32[2,256,256]{2,1,0:T(8,128)} %probe.1, ...), custom_call_target="tpu_custom_call" | custom-call | tf_op jit(solution)/shard_map/step/pallas_call | solution.py:559
  124.9 3.1 %copy.9 = f32[2,512,512]{2,1,0:T(8,128)} copy(f32[2,512,512]{2,1,0:T(8,128)} %step.1) | data formatting | bytes 4194304
  (1 shorter events, 0.0 us)
Async XLA Ops:
  2.7 1.9 %copy-start = (f32[16]{0:T(128)}, f32[16]{0:T(128)S(1)}, u32[]{:S(2)}) copy-start(f32[16]{0:T(128)S(1)} %convert_element_type.23.counts) | copy-start | bytes 196

commit v5 on v4

--- a/solution.py
+++ b/solution.py
@@ -9,6 +9,7 @@
 from jax.sharding import PartitionSpec as P
 
 STEPS = 4
+ROUNDS = 2
 
 
 KAPPA_SQ = 1.0
@@ -24,7 +25,9 @@
     cosine, sine = (np.cos(angles) * scaling, np.sin(angles) * scaling)
     ahead = np.block([[cosine, sine], [-sine, cosine]])
     conjugate = np.block([[cosine, -sine], [sine, cosine]])
-    return jnp.asarray(ahead, jnp.bfloat16), jnp.asarray(conjugate, jnp.bfloat16)
+    lines = np.arange(2 * window_cells).reshape(2, 2, ROUNDS, -1)
+    split = np.stack([conjugate[:, lines[:, :, number].reshape(-1)] for number in range(ROUNDS)])
+    return tuple(jnp.asarray(table, jnp.bfloat16) for table in (ahead, conjugate, split))
 
 
 def matmul(first, second):
@@ -34,6 +37,7 @@
 LANES = 128
 RIM = 8
 UNROLL = 6
+GRANT = 55
 MESH = pl.DeviceIdType.MESH
 ONWARD = ((1, 0), (0, 1), (1, 1))
 AROUND = ((-1, 0), (1, 0), (0, -1), (0, 1), (-1, -1), (-1, 1), (1, -1), (1, 1))
@@ -55,8 +59,10 @@
 
 
 def step_kernel(
-    sizes, slots, same, ends, counts, field, amplitudes, probe, ahead, conjugate, wide_counts, out,
-    extended, sent_rows, got_rows, staged, sent, arrived, held, passed, passed_again,
+    sizes, scan_blocks, owners, field, amplitudes, probe, ahead, conjugate, split, out,
+    slots, same, ends, counts, places, spots_of, slots_of, follows, wide_counts,
+    extended, sent_rows, got_rows, staged, sent, arrived_first, arrived_second,
+    held, passed, passed_again,
     far, phase, sums, grads, inverse, got_counts,
     sent_down, sent_right, sent_corner, got_down, got_right, got_corner,
     column_rims, got_tops, got_columns, got_corners, first_field, second_field,
@@ -113,43 +119,51 @@
             device_id_type=MESH,
         )
 
-    def piece(half, kind, first, second):
+    depth = block // ROUNDS
+    arrived = (arrived_first, arrived_second)
+    pair_slots = sent.shape[1]
+
+    def piece(half, kind, first, second, turn_of):
         a, b = place[half], place[1 - half]
-        lines = pl.ds(half * block, block)
+        inside = pl.ds(turn_of * depth, depth)
+        lines = pl.ds(half * block + turn_of * depth, depth)
+        landing = pl.ds(half * depth, depth)
         ring = 0 if kind < 4 else 1
         number = kind * SIDE + (second if ring == 0 else first)
-        sems = (send_sem.at[half, number], recv_sem.at[half, number])
+        sems = (send_sem.at[turn_of, half, number], recv_sem.at[turn_of, half, number])
         if ring == 0:
             step = 1 if kind == 0 or (kind > 1 and second < 2) else -1
             partner = owner_at(half, a + step, b)
             if kind == 3:
-                source, owner = passed.at[half, second], owner_at(half, a - step, b)
+                source, owner = passed.at[half, second, :, inside], owner_at(half, a - step, b)
             else:
                 offset = (1, -1, 2)[kind]
                 source = sent.at[owner_at(half, a + offset, b + second), :, lines]
                 owner = row
             if kind == 2:
-                target = passed.at[half, second]
+                target = passed.at[half, second, :, inside]
             elif second == 0:
-                target = arrived.at[owner, :, lines]
+                target = arrived[turn_of].at[owner, :, landing]
             else:
-                target = held.at[half, (0, 2, 2, 1)[kind], second - 1]
+                target = held.at[half, (0, 2, 2, 1)[kind], second - 1, :, inside]
         else:
             step = 1 if kind == 4 or (kind > 5 and first < 2) else -1
             partner = owner_at(half, a, b + step)
             offset = (1, 3, 2)[kind - 4] if kind < 7 else 0
             if kind == 7:
-                source = passed_again.at[half, first]
+                source = passed_again.at[half, first, :, inside]
                 owner = owner_at(half, a - first, b - step)
             else:
                 source = (
                     sent.at[owner_at(half, a, b + offset), :, lines]
                     if first == 0
-                    else held.at[half, first - 1, offset - 1]
+                    else held.at[half, first - 1, offset - 1, :, inside]
                 )
                 owner = owner_at(half, a - first, b)
             target = (
-                passed_again.at[half, first] if kind == 6 else arrived.at[owner, :, lines]
+                passed_again.at[half, first, :, inside]
+                if kind == 6
+                else arrived[turn_of].at[owner, :, landing]
             )
         return remote(source, target, sems, (partner, col))
 
@@ -172,7 +186,7 @@
         ),
     ]
 
-    halos += [
+    count_copies = [
         remote(
             wide_counts, got_counts.at[number],
             (halo_send.at[3 + number], halo_recv.at[3 + number]), around(step),
@@ -194,13 +208,22 @@
             load(number + STAGES).start()
         for half, (first, second) in enumerate(((dx, dy), (dy, dx))):
             if first:
-                piece(half, (0, 2, 1)[first - 1], None, second).start()
+                piece(half, (0, 2, 1)[first - 1], None, second, 0).start()
         if number == 6:
             for copy in halos:
                 copy.start()
 
-    own = pltpu.make_async_copy(sent.at[row], arrived.at[row], own_sem)
-    own.start()
+    own_copies = [
+        pltpu.make_async_copy(
+            sent.at[row, :, pl.ds(half * block + turn_of * depth, depth)],
+            arrived[turn_of].at[row, :, pl.ds(half * depth, depth)],
+            own_sem.at[turn_of, half],
+        )
+        for turn_of in range(ROUNDS)
+        for half in range(2)
+    ]
+    for copy in own_copies:
+        copy.start()
 
     def forward(number):
         start_row = pl.multiple_of(number // spots * block, block)
@@ -223,26 +246,86 @@
         phase[number, 0] = (far_re * inverse).astype(jnp.bfloat16)
         phase[number, 1] = (far_im * inverse).astype(jnp.bfloat16)
 
-    def relay_first():
+    def send_far():
         for second in range(SIDE):
             for half in range(2):
-                piece(half, 2, None, second).wait_recv()
-                piece(half, 3, None, second).start()
+                piece(half, 2, None, second, 1).start()
+
+    def send_near():
+        for second in (2, 1, 3, 0):
+            for kind in range(2):
+                for half in range(2):
+                    piece(half, kind, None, second, 1).start()
+
+    def relay_first(turn_of):
+        for second in range(SIDE):
+            for half in range(2):
+                piece(half, 2, None, second, turn_of).wait_recv()
+                piece(half, 3, None, second, turn_of).start()
         for kind in (6, 4, 5):
             for half in range(2):
-                piece(half, kind, 0, None).start()
-
-    def turn(first, second):
+                piece(half, kind, 0, None, turn_of).start()
+
+    def turn(first, second, turn_of):
         arrival = (0, 3, 1)[first - 1]
         kind = {1: 4, 2: 6, 3: 5}[second]
         for half in range(2):
-            piece(half, arrival, None, second).wait_recv()
-            piece(half, kind, first, None).start()
-
-    def relay_second(first):
+            piece(half, arrival, None, second, turn_of).wait_recv()
+            piece(half, kind, first, None, turn_of).start()
+
+    def relay_second(first, turn_of):
         for half in range(2):
-            piece(half, 6, first, None).wait_recv()
-            piece(half, 7, first, None).start()
+            piece(half, 6, first, None, turn_of).wait_recv()
+            piece(half, 7, first, None, turn_of).start()
+
+    def work_out_tables():
+        total = range(owners.shape[0])
+
+        def spot_of(at, carry):
+            spots_of[at] = (
+                (scan_blocks[0, at] - row * (rows // block)) * spots
+                + scan_blocks[1, at] - col * spots
+            )
+            return carry
+
+        def place_of(at, carry):
+            rank, ahead_of, matches = (jnp.zeros((), jnp.int32) for _ in range(3))
+            for other in total:
+                earlier = other < at
+                rank += jnp.where((owners[other] == owners[at]) & earlier, 1, 0)
+                ahead_of += jnp.where(spots_of[other] < spots_of[at], 1, 0)
+                matches += jnp.where((spots_of[other] == spots_of[at]) & earlier, 1, 0)
+            places[at] = ahead_of + matches
+            follows[at] = jnp.minimum(matches, 1)
+            slots_of[at] = owners[at] * pair_slots + rank
+            return carry
+
+        def sorted_at(at, carry):
+            slot, joins = (jnp.zeros((), jnp.int32) for _ in range(2))
+            for other in total:
+                slot += jnp.where(places[other] == at, slots_of[other], 0)
+                joins += jnp.where(places[other] == at, follows[other], 0)
+            slots[at] = slot
+            same[at] = joins
+            return carry
+
+        def count_at(at, carry):
+            count, up_to = (jnp.zeros((), jnp.int32) for _ in range(2))
+            for other in total:
+                count += jnp.where(spots_of[other] == at, 1, 0)
+                up_to += jnp.where(spots_of[other] <= at, 1, 0)
+            counts[at] = count.astype(jnp.float32)
+            ends[at] = jnp.maximum(up_to - 1, 0)
+            return carry
+
+        lax.fori_loop(0, len(total), spot_of, 0)
+        lax.fori_loop(0, len(total), place_of, 0)
+        lax.fori_loop(0, len(total), sorted_at, 0)
+        lax.fori_loop(0, windows, count_at, 0)
+        for number in range(windows):
+            wide_counts[number : number + 1, :] = jnp.full((1, LANES), counts[number])
+        for copy in count_copies:
+            copy.start()
 
     def take_halos():
         for copy in halos:
@@ -287,13 +370,17 @@
 
     inner = spots - 1
     steps = {
-        3: [relay_first],
-        5: [functools.partial(turn, 1, 2)],
-        7: [functools.partial(turn, 3, 2), take_halos],
-        9: [functools.partial(turn, 1, 1)],
-        11: [functools.partial(turn, 3, 1)],
-        13: [functools.partial(turn, 1, 3)],
-        14: [functools.partial(turn, 3, 3)],
+        3: [functools.partial(relay_first, 0)],
+        5: [functools.partial(turn, 1, 2, 0)],
+        6: [send_far],
+        7: [functools.partial(turn, 3, 2, 0), take_halos],
+        8: [send_near],
+        9: [functools.partial(turn, 1, 1, 0)],
+        10: [functools.partial(turn, 3, 1, 0)],
+        11: [functools.partial(turn, 1, 3, 0)],
+        12: [functools.partial(turn, 3, 3, 0)],
+        13: [functools.partial(relay_first, 1)],
+        14: [functools.partial(turn, 2, 2, 0)],
     }
 
     def forward_step(index, carry):
@@ -312,30 +399,22 @@
         return carry
 
     lax.fori_loop(0, windows, forward_step, 0)
+    work_out_tables()
+    for second in (1, 3):
+        turn(2, second, 0)
+    for first in (0, 1, 3, 2):
+        relay_second(first, 0)
     for second in (2, 1, 3):
-        turn(2, second)
+        for first in (1, 3):
+            turn(first, second, 1)
     grads[...] = jnp.zeros_like(grads)
-    for first in (0, 1, 3):
-        relay_second(first)
+    for second in (2, 1, 3):
+        turn(2, second, 1)
+    for copy in count_copies:
+        copy.wait()
     light_up()
-    relay_second(2)
-
-    own.wait()
-    for half in range(2):
-        for kind in (0, 1, 3):
-            piece(half, kind, None, 0).wait_recv()
-        for kind in (4, 5, 7):
-            for first in range(SIDE):
-                piece(half, kind, first, None).wait_recv()
-
-    def add_up(index, carry):
-        slot = slots[index]
-        plane = arrived[slot // arrived.shape[1], lax.rem(slot, arrived.shape[1])]
-        before = jnp.where(same[index] > 0, sums[jnp.maximum(index - 1, 0)], 0.0)
-        sums[index] = before + plane.astype(jnp.float32)
-        return carry
-
-    lax.fori_loop(0, sums.shape[0], add_up, 0)
+    for copy in own_copies:
+        copy.wait()
 
     sum_copies = [
         remote(source, target, (sum_send.at[number], sum_recv.at[number]), around(ONWARD[number]))
@@ -344,7 +423,45 @@
         )
     ]
 
-    def backward(index, carry):
+    def round_lines(turn_of):
+        return [
+            pl.ds(pl.multiple_of(half * block + turn_of * depth, depth), depth)
+            for half in range(2)
+        ]
+
+    def add_up(turn_of, index, carry):
+        slot = slots[index]
+        owner, rank = slot // pair_slots, lax.rem(slot, pair_slots)
+        for half, lines in enumerate(round_lines(turn_of)):
+            before = jnp.where(same[index] > 0, sums[jnp.maximum(index - 1, 0), lines], 0.0)
+            plane = arrived[turn_of][owner, rank, pl.ds(half * depth, depth)]
+            sums[index, lines] = before + plane.astype(jnp.float32)
+        return carry
+
+    def take_round(turn_of):
+        for half in range(2):
+            for kind in (0, 1, 3):
+                piece(half, kind, None, 0, turn_of).wait_recv()
+            for kind in (4, 5, 7):
+                for first in range(SIDE):
+                    piece(half, kind, first, None, turn_of).wait_recv()
+        lax.fori_loop(0, sums.shape[0], functools.partial(add_up, turn_of), 0)
+
+    def backward(step, carry):
+        turn_of, index = step // windows, lax.rem(step, windows)
+
+        for number in range(ROUNDS):
+
+            @pl.when(step == number * windows)
+            def _(number=number):
+                take_round(number)
+
+        for when, first in ((2, 0), (4, 1), (7, 3), (10, 2)):
+
+            @pl.when(step == when)
+            def _(first=first):
+                relay_second(first, 1)
+
         interior = index - 2 * spots + 1
         edge = interior < 0
         at_row = jnp.where(
@@ -355,7 +472,7 @@
         )
         number = at_row * spots + at_col
 
-        @pl.when(index == 2 * spots - 1)
+        @pl.when(step == windows + 2 * spots - 1)
         def _():
             sent_down[...] = grads[:, rows:, :cols].astype(jnp.bfloat16)
             sent_right[...] = grads[:, :rows, cols:].astype(jnp.bfloat16)
@@ -364,17 +481,21 @@
                 copy.start()
 
         count = counts[number]
-        total = sums[ends[number]] * jnp.minimum(count, 1.0)
-        residual = [
-            (
-                far[number, part].astype(jnp.float32) * count
-                - phase[number, part].astype(jnp.float32) * total
-            ).astype(jnp.bfloat16)
-            for part in range(2)
-        ]
-        back = matmul(conjugate[...], jnp.concatenate(residual, axis=0)).astype(jnp.bfloat16)
-        near = matmul(jnp.concatenate([back[:cells], back[cells:]], axis=1), ahead[...])
-        near_re, near_im = near[:, :cells], near[:, cells:]
+        used = jnp.minimum(count, 1.0)
+        last = ends[number]
+        parts = []
+        for part in range(2):
+            pieces = [
+                far[number, part, lines].astype(jnp.float32) * count
+                - phase[number, part, lines].astype(jnp.float32) * (sums[last, lines] * used)
+                for lines in round_lines(turn_of)
+            ]
+            parts.append(jnp.concatenate(pieces, axis=0).astype(jnp.bfloat16))
+        across = matmul(jnp.concatenate(parts, axis=1), ahead[...]).astype(jnp.bfloat16)
+        near = matmul(
+            split[turn_of], jnp.concatenate([across[:, :cells], across[:, cells:]], axis=0)
+        )
+        near_re, near_im = near[:cells], near[cells:]
         probe_re, probe_im = probe[0], probe[1]
         view = (
             pl.ds(pl.multiple_of(at_row * block, block), cells),
@@ -384,7 +505,7 @@
         grads[(1, *view)] += probe_re * near_im - probe_im * near_re
         return carry
 
-    lax.fori_loop(0, windows, backward, 0)
+    lax.fori_loop(0, ROUNDS * windows, backward, 0)
     strips = cols // LANES
     for copy in sum_copies:
         copy.wait()
@@ -530,16 +651,17 @@
         now, later = later, now
     smooth(now, give, 0, chunks - 1)
 
-    for half in range(2):
-        for kind in range(4):
-            for second in range(SIDE):
-                piece(half, kind, None, second).wait_send()
-        for kind in range(4, 8):
-            for first in range(SIDE):
-                piece(half, kind, first, None).wait_send()
-
-
-def whole_step(object_field, probe_field, amplitudes, tables, scalars, wide_counts):
+    for turn_of in range(ROUNDS):
+        for half in range(2):
+            for kind in range(4):
+                for second in range(SIDE):
+                    piece(half, kind, None, second, turn_of).wait_send()
+            for kind in range(4, 8):
+                for first in range(SIDE):
+                    piece(half, kind, first, None, turn_of).wait_send()
+
+
+def whole_step(object_field, probe_field, amplitudes, scan_blocks, owner_rows):
     rows, cols = object_field.shape[1:]
     cells = probe_field.shape[1]
     block = cells // 2
@@ -547,6 +669,7 @@
     groups = lax.axis_size("tx")
     slots = amplitudes.shape[0] // groups
     sizes = (groups, lax.axis_size("ty"))
+    positions = owner_rows.shape[0]
     assert groups == SIDE * SIDE
     vmem = pl.BlockSpec(memory_space=pltpu.VMEM)
     smem = pl.BlockSpec(memory_space=pltpu.SMEM)
@@ -559,24 +682,32 @@
     return pl.pallas_call(
         functools.partial(step_kernel, sizes),
         out_shape=jax.ShapeDtypeStruct(object_field.shape, wide),
-        in_specs=[smem] * 4 + [anywhere] * 2 + [vmem] * 4,
+        in_specs=[smem] * 2 + [anywhere] * 2 + [vmem] * 4,
         out_specs=vmem,
         scratch_shapes=[
+            *(
+                pltpu.SMEM((length,), kind)
+                for length, kind in (
+                    (positions, jnp.int32), (positions, jnp.int32), (windows, jnp.int32),
+                    (windows, wide), *((positions, jnp.int32) for _ in range(4)),
+                )
+            ),
+            pltpu.VMEM((windows, LANES), wide),
             pltpu.VMEM((2, rows + block, cols + block), wide),
             pltpu.VMEM((2, block, cols), narrow),
             pltpu.VMEM((2, block, cols), narrow),
             pltpu.VMEM((STAGES, slots, cells, cells), wide),
             pltpu.VMEM(own, narrow),
-            pltpu.VMEM(own, narrow),
+            *(pltpu.VMEM((groups, slots, cells // ROUNDS, cells), narrow) for _ in range(ROUNDS)),
             pltpu.VMEM((2, SIDE - 1, SIDE - 1, *part), narrow),
             pltpu.VMEM((2, SIDE, *part), narrow),
             pltpu.VMEM((2, SIDE, *part), narrow),
             pltpu.VMEM((windows, 2, cells, cells), narrow),
             pltpu.VMEM((windows, 2, cells, cells), narrow),
-            pltpu.VMEM((scalars[0].shape[0], cells, cells), wide),
+            pltpu.VMEM((positions, cells, cells), wide),
             pltpu.VMEM((2, rows + block, cols + block), wide),
             pltpu.VMEM((rows, cols), wide),
-            pltpu.VMEM((3, *wide_counts.shape), wide),
+            pltpu.VMEM((3, windows, LANES), wide),
             *(pltpu.VMEM(strip, narrow) for strip in strips * 2),
             pltpu.VMEM((2, 2, RIM, rows), wide),
             pltpu.VMEM((2, 2, cols // LANES, RIM, LANES), wide),
@@ -586,61 +717,24 @@
             pltpu.VMEM(smoothed, wide),
             pltpu.SemaphoreType.DMA((STAGES,)),
             pltpu.SemaphoreType.DMA,
-            pltpu.SemaphoreType.DMA,
+            pltpu.SemaphoreType.DMA((ROUNDS, 2)),
             pltpu.SemaphoreType.DMA((6,)),
             pltpu.SemaphoreType.DMA((6,)),
-            pltpu.SemaphoreType.DMA((2, 8 * SIDE)),
-            pltpu.SemaphoreType.DMA((2, 8 * SIDE)),
+            pltpu.SemaphoreType.DMA((ROUNDS, 2, 8 * SIDE)),
+            pltpu.SemaphoreType.DMA((ROUNDS, 2, 8 * SIDE)),
             pltpu.SemaphoreType.DMA((3,)),
             pltpu.SemaphoreType.DMA((3,)),
             pltpu.SemaphoreType.DMA((8,)),
             pltpu.SemaphoreType.DMA((8,)),
         ],
         compiler_params=pltpu.CompilerParams(
-            collective_id=1, has_side_effects=True, vmem_limit_bytes=60 << 20
+            collective_id=1, has_side_effects=True, vmem_limit_bytes=GRANT << 20
         ),
         name="step",
     )(
-        *scalars, object_field, amplitudes.reshape(own), probe_field, *tables, wide_counts
+        scan_blocks.T, owner_rows, object_field, amplitudes.reshape(own), probe_field,
+        *complex_tables(cells)
     )
-
-
-def local(object_field, probe_field, amplitudes, scan_blocks, owner_rows):
-    tile_rows, tile_cols = object_field.shape[1:]
-    window_cells = probe_field.shape[1]
-    block_cells = window_cells // 2
-    positions_here = owner_rows.shape[0]
-    pair_slots = amplitudes.shape[0] // lax.axis_size("tx")
-    spots = tile_cols // block_cells
-    windows = tile_rows // block_cells * spots
-
-    order = jnp.arange(positions_here, dtype=jnp.int32)
-    earlier = order[None, :] < order[:, None]
-    pair_rank = jnp.sum((owner_rows[:, None] == owner_rows[None, :]) & earlier, axis=1)
-    slot_index = owner_rows * pair_slots + pair_rank.astype(jnp.int32)
-    window_index = (
-        (scan_blocks[:, 0] - lax.axis_index("tx") * (tile_rows // block_cells)) * spots
-        + scan_blocks[:, 1] - lax.axis_index("ty") * spots
-    )
-    before = (window_index[None, :] < window_index[:, None]) | (
-        (window_index[None, :] == window_index[:, None]) & earlier
-    )
-    place = jnp.sum(before, axis=1)
-    slots = jnp.sum(
-        jnp.where(place[None, :] == order[:, None], slot_index[None, :], 0), axis=1
-    ).astype(jnp.int32)
-    bounds = jnp.arange(windows, dtype=jnp.int32)
-    counts = jnp.sum(window_index[None, :] == bounds[:, None], axis=1).astype(jnp.float32)
-    ends = jnp.sum(window_index[None, :] <= bounds[:, None], axis=1).astype(jnp.int32)
-    follows = (window_index[None, :] == window_index[:, None]) & earlier
-    same = jnp.sum(
-        jnp.where(place[None, :] == order[:, None], jnp.any(follows, axis=1)[None, :], False),
-        axis=1,
-    ).astype(jnp.int32)
-    scalars = (slots, same, jnp.maximum(ends - 1, 0), counts)
-    wide_counts = jnp.broadcast_to(counts[:, None], (windows, LANES))
-    tables = complex_tables(window_cells)
-    return whole_step(object_field, probe_field, amplitudes, tables, scalars, wide_counts)
 
 
 def solution(mesh):
@@ -652,4 +746,4 @@
         P(("tx", "ty")),
     )
     out_specs = P(None, "tx", "ty")
-    return jax.shard_map(local, mesh=mesh, in_specs=in_specs, out_specs=out_specs, check_vma=False)
+    return jax.shard_map(whole_step, mesh=mesh, in_specs=in_specs, out_specs=out_specs, check_vma=False)

time: 130 us -> 125 us (0.962)
  other arithmetic: 3.88 us -> 0 us
    reduce_sum x3 -> x0, other arithmetic: 1.75 us -> none  [the longest x1 0.91 us: local(): jnp.sum((owner_rows[:, None] == owner_rows[None, :]) & earlier, axis=1)]
    unnamed x3 -> x1, local copies, waits for them, and re-layouts: 3.08 us -> 3.08 us
where the time goes in v5:
time: 125 us; the launch traced here: 123 us
  Pallas kernels  120 us (96%)
  local copies, waits for them, and re-layouts  3.08 us (2%)
    pallas_call x1, Pallas kernels, whole_step(): pl.pallas_call(functools.partial(step_kernel, sizes), out_shape=jax.Shape...  120 us
    unnamed x1, local copies, waits for them, and re-layouts  3.08 us

profile of v5, /device:TPU:7, one launch (start us, length us, event | category | flops | bytes accessed | tf_op | source)
XLA Modules:
  0.0 123.0 jit_solution(2138982641039018260)
XLA Ops:
  0.0 119.9 %step.1 = f32[2,512,512]{2,1,0:T(8,128)} custom-call(s32[2,16]{1,0:T(2,128)} %bitcast.3, s32[16]{0:T(128)} %owners.1, f32[2,512,512]{2,1,0:T(8,128)} %field.1, f32[16,3,256,256]{3,2,1,0:T(8,128)} %bitcast.2, f32[2,256,256]{2,1,0:T(8,128)} %probe.1, bf16[512,512]{1,0:T(8,128)(2,1)} %constant.6.clone.ahead, bf16[512,512]{1,0:T(8,128)(2,1)} %constant.7.clone.conjugate, ...), custom_call_target="tpu_custom_call" | custom-call | tf_op jit(solution)/shard_map/step/pallas_call | solution.py:682
  119.9 3.1 %copy.10 = f32[2,512,512]{2,1,0:T(8,128)} copy(f32[2,512,512]{2,1,0:T(8,128)} %step.1) | data formatting | bytes 4194304

commit v6 on v5

--- a/solution.py
+++ b/solution.py
@@ -37,7 +37,7 @@
 LANES = 128
 RIM = 8
 UNROLL = 6
-GRANT = 55
+GRANT = 49
 MESH = pl.DeviceIdType.MESH
 ONWARD = ((1, 0), (0, 1), (1, 1))
 AROUND = ((-1, 0), (1, 0), (0, -1), (0, 1), (-1, -1), (-1, 1), (1, -1), (1, 1))
@@ -49,7 +49,7 @@
 
 
 SIDE = 4
-STAGES = 4
+STAGES = 2
 TAKEN = tuple(
     sorted(
         ((dx, dy) for dx in range(SIDE) for dy in range(SIDE)),
@@ -59,14 +59,15 @@
 
 
 def step_kernel(
-    sizes, scan_blocks, owners, field, amplitudes, probe, ahead, conjugate, split, out,
+    sizes, scan_blocks, owners, field, amplitudes, probe_given, ahead_given, conjugate_given,
+    split_given, out, probe, ahead, conjugate, split,
     slots, same, ends, counts, places, spots_of, slots_of, follows, wide_counts,
     extended, sent_rows, got_rows, staged, sent, arrived_first, arrived_second,
     held, passed, passed_again,
     far, phase, sums, grads, inverse, got_counts,
-    sent_down, sent_right, sent_corner, got_down, got_right, got_corner,
+    sent_right, sent_corner, got_down, got_right, got_corner,
     column_rims, got_tops, got_columns, got_corners, first_field, second_field,
-    stage_sem, field_sem, own_sem, halo_send, halo_recv, send_sem, recv_sem,
+    stage_sem, field_sem, table_sem, own_sem, halo_send, halo_recv, send_sem, recv_sem,
     sum_send, sum_recv, rim_send, rim_recv,
 ):
     n_tx, n_ty = sizes
@@ -96,9 +97,18 @@
     take_field = pltpu.make_async_copy(
         field, extended.at[:, pl.ds(0, rows), pl.ds(0, cols)], field_sem
     )
-    take_field.start()
+    take_tables = [
+        pltpu.make_async_copy(source, target, table_sem.at[number])
+        for number, (source, target) in enumerate(
+            (
+                (probe_given, probe), (ahead_given, ahead), (conjugate_given, conjugate),
+                (split_given, split),
+            )
+        )
+    ]
     for number in range(STAGES):
         load(number).start()
+    take_field.start()
 
     barrier = pltpu.get_barrier_semaphore()
     partners = [around(step) for step in AROUND] + [
@@ -132,7 +142,8 @@
         number = kind * SIDE + (second if ring == 0 else first)
         sems = (send_sem.at[turn_of, half, number], recv_sem.at[turn_of, half, number])
         if ring == 0:
-            step = 1 if kind == 0 or (kind > 1 and second < 2) else -1
+            upward = 3 if (half, turn_of) == (1, 0) else 2
+            step = 1 if kind == 0 or (kind > 1 and second < upward) else -1
             partner = owner_at(half, a + step, b)
             if kind == 3:
                 source, owner = passed.at[half, second, :, inside], owner_at(half, a - step, b)
@@ -167,10 +178,6 @@
             )
         return remote(source, target, sems, (partner, col))
 
-    take_field.wait()
-    sent_rows[...] = extended[:, :block, :cols].astype(jnp.bfloat16)
-    pl.semaphore_wait(barrier, len(partners))
-
     corner = (pl.ds(rows, block), pl.ds(cols, block))
     halos = [
         remote(sent_rows, got_rows, (halo_send.at[0], halo_recv.at[0]), around((-1, 0))),
@@ -204,11 +211,18 @@
             return carry
 
         lax.fori_loop(0, sent.shape[1], cast, 0)
+        if number == 0:
+            pl.semaphore_wait(barrier, len(partners))
         if number + STAGES < len(TAKEN):
             load(number + STAGES).start()
         for half, (first, second) in enumerate(((dx, dy), (dy, dx))):
             if first:
                 piece(half, (0, 2, 1)[first - 1], None, second, 0).start()
+        if number == 4:
+            for copy in take_tables:
+                copy.start()
+            take_field.wait()
+            sent_rows[...] = extended[:, :block, :cols].astype(jnp.bfloat16)
         if number == 6:
             for copy in halos:
                 copy.start()
@@ -382,6 +396,9 @@
         13: [functools.partial(relay_first, 1)],
         14: [functools.partial(turn, 2, 2, 0)],
     }
+
+    for copy in take_tables:
+        copy.wait()
 
     def forward_step(index, carry):
         edge = index - inner * inner
@@ -419,7 +436,7 @@
     sum_copies = [
         remote(source, target, (sum_send.at[number], sum_recv.at[number]), around(ONWARD[number]))
         for number, (source, target) in enumerate(
-            ((sent_down, got_down), (sent_right, got_right), (sent_corner, got_corner))
+            ((sent_rows, got_down), (sent_right, got_right), (sent_corner, got_corner))
         )
     ]
 
@@ -472,13 +489,17 @@
         )
         number = at_row * spots + at_col
 
+        @pl.when(step == windows + spots)
+        def _():
+            sent_rows[...] = grads[:, rows:, :cols].astype(jnp.bfloat16)
+            sent_corner[...] = grads[:, rows:, cols:].astype(jnp.bfloat16)
+            sum_copies[2].start()
+            sum_copies[0].start()
+
         @pl.when(step == windows + 2 * spots - 1)
         def _():
-            sent_down[...] = grads[:, rows:, :cols].astype(jnp.bfloat16)
             sent_right[...] = grads[:, :rows, cols:].astype(jnp.bfloat16)
-            sent_corner[...] = grads[:, rows:, cols:].astype(jnp.bfloat16)
-            for copy in sum_copies:
-                copy.start()
+            sum_copies[1].start()
 
         count = counts[number]
         used = jnp.minimum(count, 1.0)
@@ -670,10 +691,11 @@
     slots = amplitudes.shape[0] // groups
     sizes = (groups, lax.axis_size("ty"))
     positions = owner_rows.shape[0]
+    tables = complex_tables(cells)
     assert groups == SIDE * SIDE
     vmem = pl.BlockSpec(memory_space=pltpu.VMEM)
     smem = pl.BlockSpec(memory_space=pltpu.SMEM)
-    anywhere = pl.BlockSpec(memory_space=pl.ANY)
+    anywhere = pl.BlockSpec(memory_space=pltpu.HBM)
     narrow, wide = jnp.bfloat16, jnp.float32
     own = (groups, slots, cells, cells)
     part = (slots, block, cells)
@@ -682,9 +704,11 @@
     return pl.pallas_call(
         functools.partial(step_kernel, sizes),
         out_shape=jax.ShapeDtypeStruct(object_field.shape, wide),
-        in_specs=[smem] * 2 + [anywhere] * 2 + [vmem] * 4,
+        in_specs=[smem] * 2 + [anywhere] * 6,
         out_specs=vmem,
         scratch_shapes=[
+            pltpu.VMEM(probe_field.shape, wide),
+            *(pltpu.VMEM(table.shape, narrow) for table in tables),
             *(
                 pltpu.SMEM((length,), kind)
                 for length, kind in (
@@ -708,7 +732,7 @@
             pltpu.VMEM((2, rows + block, cols + block), wide),
             pltpu.VMEM((rows, cols), wide),
             pltpu.VMEM((3, windows, LANES), wide),
-            *(pltpu.VMEM(strip, narrow) for strip in strips * 2),
+            *(pltpu.VMEM(strip, narrow) for strip in strips[1:] + strips),
             pltpu.VMEM((2, 2, RIM, rows), wide),
             pltpu.VMEM((2, 2, cols // LANES, RIM, LANES), wide),
             pltpu.VMEM((2, 2, RIM, rows), wide),
@@ -717,6 +741,7 @@
             pltpu.VMEM(smoothed, wide),
             pltpu.SemaphoreType.DMA((STAGES,)),
             pltpu.SemaphoreType.DMA,
+            pltpu.SemaphoreType.DMA((4,)),
             pltpu.SemaphoreType.DMA((ROUNDS, 2)),
             pltpu.SemaphoreType.DMA((6,)),
             pltpu.SemaphoreType.DMA((6,)),
@@ -733,7 +758,7 @@
         name="step",
     )(
         scan_blocks.T, owner_rows, object_field, amplitudes.reshape(own), probe_field,
-        *complex_tables(cells)
+        *tables
     )
 
 

time: 125 us -> 124 us (level)
  Pallas kernels: 120 us -> 116 us
  local copies, waits for them, and re-layouts: 3.08 us -> 6.82 us
    unnamed x1 -> x13, local copies, waits for them, and re-layouts: 3.08 us -> 6.82 us
    pallas_call x1, Pallas kernels: 120 us -> 116 us  [whole_step(): pl.pallas_call(functools.partial(step_kernel, sizes), out_shape=jax.Shape...]
where the time goes in v6:
time: 124 us; the launch traced here: 123 us
  Pallas kernels  116 us (94%)
  local copies, waits for them, and re-layouts  6.82 us (6%)
    pallas_call x1, Pallas kernels, whole_step(): pl.pallas_call(functools.partial(step_kernel, sizes), out_shape=jax.Shape...  116 us
    unnamed x13, local copies, waits for them, and re-layouts  6.82 us

profile of v6, /device:TPU:7, one launch (start us, length us, event | category | flops | bytes accessed | tf_op | source)
XLA Modules:
  0.0 123.2 jit_solution(16163332024037377469)
XLA Ops:
  0.0 0.0 copy-start
  0.0 1.0 copy-done
  1.0 0.0 copy-start.1
  1.0 1.0 copy-done.1
  2.1 0.0 copy-start.2
  2.1 1.0 copy-done.2
  3.1 0.0 copy-start.3
  3.1 1.0 copy-done.3
  4.2 0.0 copy-start.4
  4.2 0.7 copy-done.4
  4.8 0.0 copy-start.5
  4.9 0.7 copy-done.5
  5.5 116.4 %step.1 = f32[2,512,512]{2,1,0:T(8,128)S(1)} custom-call(s32[2,16]{1,0:T(2,128)S(1)} %bitcast.2, s32[16]{0:T(128)S(1)} %copy-done.5, f32[2,512,512]{2,1,0:T(8,128)} %field.1, f32[16,3,256,256]{3,2,1,0:T(8,128)} %bitcast.3, f32[2,256,256]{2,1,0:T(8,128)S(1)} %copy-done, bf16[512,512]{1,0:T(8,128)(2,1)S(1)} %copy-done.3, bf16[512,512]{1,0:T(8,128)(2,1)S(1)} %copy-done.2, ...), custom_call_target="tpu_custom_call" | custom-call | tf_op jit(solution)/shard_map/step/pallas_call | solution.py:704
  121.9 1.3 %copy.10 = f32[2,512,512]{2,1,0:T(8,128)} copy(f32[2,512,512]{2,1,0:T(8,128)S(1)} %step.1) | data formatting | bytes 4194304
Async XLA Ops:
  0.0 1.0 copy-start
  1.0 1.0 copy-start.1
  2.1 1.0 copy-start.2
  3.1 1.0 copy-start.3
  4.2 0.7 copy-start.4
  4.8 0.7 copy-start.5

commit v7 on v6

--- a/solution.py
+++ b/solution.py
@@ -37,7 +37,7 @@
 LANES = 128
 RIM = 8
 UNROLL = 6
-GRANT = 49
+GRANT = 55
 MESH = pl.DeviceIdType.MESH
 ONWARD = ((1, 0), (0, 1), (1, 1))
 AROUND = ((-1, 0), (1, 0), (0, -1), (0, 1), (-1, -1), (-1, 1), (1, -1), (1, 1))
@@ -49,7 +49,7 @@
 
 
 SIDE = 4
-STAGES = 2
+STAGES = 3
 TAKEN = tuple(
     sorted(
         ((dx, dy) for dx in range(SIDE) for dy in range(SIDE)),
@@ -266,17 +266,24 @@
                 piece(half, 2, None, second, 1).start()
 
     def send_near():
-        for second in (2, 1, 3, 0):
+        for second in (2, 1, 3):
             for kind in range(2):
                 for half in range(2):
                     piece(half, kind, None, second, 1).start()
+
+    def send_last():
+        for half in range(2):
+            for kind in range(2):
+                piece(half, kind, None, 0, 1).start()
+            for kind in (4, 5):
+                piece(half, kind, 0, None, 1).start()
 
     def relay_first(turn_of):
         for second in range(SIDE):
             for half in range(2):
                 piece(half, 2, None, second, turn_of).wait_recv()
                 piece(half, 3, None, second, turn_of).start()
-        for kind in (6, 4, 5):
+        for kind in (6,) if turn_of == ROUNDS - 1 else (6, 4, 5):
             for half in range(2):
                 piece(half, kind, 0, None, turn_of).start()
 
@@ -427,6 +434,7 @@
     grads[...] = jnp.zeros_like(grads)
     for second in (2, 1, 3):
         turn(2, second, 1)
+    send_last()
     for copy in count_copies:
         copy.wait()
     light_up()
@@ -528,23 +536,26 @@
 
     lax.fori_loop(0, ROUNDS * windows, backward, 0)
     strips = cols // LANES
+
+    def refresh(part, strip, start, count):
+        lines, lanes = pl.ds(start, count), pl.ds(strip * LANES, LANES)
+        updated = (
+            extended[part, lines, lanes] - grads[part, lines, lanes] * inverse[lines, lanes]
+        )
+        first_field[part, strip, pl.ds(2 * RIM + start, count), :] = updated
+        return updated
+
     for copy in sum_copies:
         copy.wait()
     for part in range(2):
         grads[part, :block, :cols] += got_down[part].astype(jnp.float32) * above
         grads[part, :rows, :block] += got_right[part].astype(jnp.float32) * left
         grads[part, :block, :block] += got_corner[part].astype(jnp.float32) * (above * left)
-        for strip in range(strips):
-            lanes = pl.ds(strip * LANES, LANES)
-            updated = (
-                extended[part, pl.ds(0, rows), lanes]
-                - grads[part, pl.ds(0, rows), lanes] * inverse[:, lanes]
-            )
-            first_field[part, strip, pl.ds(2 * RIM, rows), :] = updated
-            if strip == 0:
-                column_rims[0, part] = updated.T[:RIM]
-            if strip == strips - 1:
-                column_rims[1, part] = updated.T[LANES - RIM :]
+        column_rims[0, part] = refresh(part, 0, 0, rows).T[:RIM]
+        column_rims[1, part] = refresh(part, strips - 1, 0, rows).T[LANES - RIM :]
+        for strip in range(1, strips - 1):
+            for start in (0, rows - RIM):
+                refresh(part, strip, start, RIM)
 
     top, bottom = pl.ds(2 * RIM, RIM), pl.ds(2 * RIM + rows - RIM, RIM)
     main = pl.ds(0, strips)
@@ -565,6 +576,9 @@
     ]
     for copy in rim_copies:
         copy.start()
+    for part in range(2):
+        for strip in range(1, strips - 1):
+            refresh(part, strip, RIM, rows - 2 * RIM)
     for copy in rim_copies:
         copy.wait()
 

time: 124 us -> 120 us (0.968)
  local copies, waits for them, and re-layouts: 6.82 us -> 3.08 us
    unnamed x13 -> x1, local copies, waits for them, and re-layouts: 6.82 us -> 3.08 us
where the time goes in v7:
time: 120 us
  Pallas kernels  117 us (98%)
  local copies, waits for them, and re-layouts  3.08 us (3%)
    pallas_call x1, Pallas kernels, whole_step(): pl.pallas_call(functools.partial(step_kernel, sizes), out_shape=jax.Shape...  117 us
    unnamed x1, local copies, waits for them, and re-layouts  3.08 us

profile of v7, /device:TPU:7, one launch (start us, length us, event | category | flops | bytes accessed | tf_op | source)
XLA Modules:
  0.0 119.8 jit_solution(16996378138723559552)
XLA Ops:
  0.0 116.7 %step.1 = f32[2,512,512]{2,1,0:T(8,128)} custom-call(s32[2,16]{1,0:T(2,128)} %bitcast.3, s32[16]{0:T(128)} %owners.1, f32[2,512,512]{2,1,0:T(8,128)} %field.1, f32[16,3,256,256]{3,2,1,0:T(8,128)} %bitcast.2, f32[2,256,256]{2,1,0:T(8,128)} %probe_given.1, bf16[512,512]{1,0:T(8,128)(2,1)} %constant.6.clone.ahead_given, ...), custom_call_target="tpu_custom_call" | custom-call | tf_op jit(solution)/shard_map/step/pallas_call | solution.py:718
  116.7 3.1 %copy.10 = f32[2,512,512]{2,1,0:T(8,128)} copy(f32[2,512,512]{2,1,0:T(8,128)} %step.1) | data formatting | bytes 4194304

commit v8 on v7

--- a/solution.py
+++ b/solution.py
@@ -441,11 +441,14 @@
     for copy in own_copies:
         copy.wait()
 
+    across_blocks = [pl.ds(number * block, block) for number in range(spots)]
+    ways = [(sent_right, got_right, ONWARD[1]), (sent_corner, got_corner, ONWARD[2])] + [
+        (sent_rows.at[:, :, lanes], got_down.at[:, :, lanes], ONWARD[0])
+        for lanes in across_blocks
+    ]
     sum_copies = [
-        remote(source, target, (sum_send.at[number], sum_recv.at[number]), around(ONWARD[number]))
-        for number, (source, target) in enumerate(
-            ((sent_rows, got_down), (sent_right, got_right), (sent_corner, got_corner))
-        )
+        remote(source, target, (sum_send.at[number], sum_recv.at[number]), around(step))
+        for number, (source, target, step) in enumerate(ways)
     ]
 
     def round_lines(turn_of):
@@ -497,17 +500,22 @@
         )
         number = at_row * spots + at_col
 
+        for part, lanes in enumerate(across_blocks):
+
+            @pl.when(step == windows + part + 1)
+            def _(part=part, lanes=lanes):
+                sent_rows[:, :, lanes] = grads[:, rows:, lanes].astype(jnp.bfloat16)
+                sum_copies[2 + part].start()
+
         @pl.when(step == windows + spots)
         def _():
-            sent_rows[...] = grads[:, rows:, :cols].astype(jnp.bfloat16)
             sent_corner[...] = grads[:, rows:, cols:].astype(jnp.bfloat16)
-            sum_copies[2].start()
-            sum_copies[0].start()
+            sum_copies[1].start()
 
         @pl.when(step == windows + 2 * spots - 1)
         def _():
             sent_right[...] = grads[:, :rows, cols:].astype(jnp.bfloat16)
-            sum_copies[1].start()
+            sum_copies[0].start()
 
         count = counts[number]
         used = jnp.minimum(count, 1.0)
@@ -761,8 +769,8 @@
             pltpu.SemaphoreType.DMA((6,)),
             pltpu.SemaphoreType.DMA((ROUNDS, 2, 8 * SIDE)),
             pltpu.SemaphoreType.DMA((ROUNDS, 2, 8 * SIDE)),
-            pltpu.SemaphoreType.DMA((3,)),
-            pltpu.SemaphoreType.DMA((3,)),
+            pltpu.SemaphoreType.DMA((2 + cols // block,)),
+            pltpu.SemaphoreType.DMA((2 + cols // block,)),
             pltpu.SemaphoreType.DMA((8,)),
             pltpu.SemaphoreType.DMA((8,)),
         ],

time: 120 us -> 119 us (level)
  no operation moved by 1% of the time
where the time goes in v8:
time: 119 us
  Pallas kernels  116 us (97%)
  local copies, waits for them, and re-layouts  3.08 us (3%)
    pallas_call x1, Pallas kernels, whole_step(): pl.pallas_call(functools.partial(step_kernel, sizes), out_shape=jax.Shape...  116 us
    unnamed x1, local copies, waits for them, and re-layouts  3.08 us

profile of v8, /device:TPU:7, one launch (start us, length us, event | category | flops | bytes accessed | tf_op | source)
XLA Modules:
  0.0 118.7 jit_solution(96562540393480814)
XLA Ops:
  0.0 115.6 %step.1 = f32[2,512,512]{2,1,0:T(8,128)} custom-call(s32[2,16]{1,0:T(2,128)} %bitcast.3, s32[16]{0:T(128)} %owners.1, f32[2,512,512]{2,1,0:T(8,128)} %field.1, f32[16,3,256,256]{3,2,1,0:T(8,128)} %bitcast.2, f32[2,256,256]{2,1,0:T(8,128)} %probe_given.1, bf16[512,512]{1,0:T(8,128)(2,1)} %constant.6.clone.ahead_given, ...), custom_call_target="tpu_custom_call" | custom-call | tf_op jit(solution)/shard_map/step/pallas_call | solution.py:726
  115.6 3.1 %copy.10 = f32[2,512,512]{2,1,0:T(8,128)} copy(f32[2,512,512]{2,1,0:T(8,128)} %step.1) | data formatting | bytes 4194304
